TPU v7x, 256 devices: a whole 4x4x8 slice. The times are simulated.
256 devices in a mesh: grp: 8 (over z_lo, y), sub: 32 (over z_hi, x, core).
Axes of the slice: x: 4, y: 4, z: 8 (z_hi: 4, z_lo: 2; z = z_hi * 2 + z_lo), core: 2. Of those that a mesh axis runs over, the one named last changes fastest.
Arguments:
- right_side: float32 [16, 128, 512, 128], P(None, 'grp', 'sub'), may hold values from -12 to 12
- conductivity: float32 [128, 512, 128], P('grp', 'sub'), may hold values from 0.1 to 10
- pinned_cells: int32 [128, 512, 128], P('grp', 'sub'), may hold values 0 or 1
- coarse_basis: float32 [32, 128, 512, 128], P(None, 'grp', 'sub'), may hold values from -0.03125 to 0.03125
- coarse_inverse: float32 [8, 1024, 8192], P(None, 'sub', 'grp'), as said below
Outputs:
- solution: float32 [16, 128, 512, 128], P(None, 'grp', 'sub')
- residual: float32 [16, 128, 512, 128], P(None, 'grp', 'sub')
Inputs may be any that keep to these rules, and one draw needn't show every extreme that they name: coarse_inverse is symmetric as a 8192 x 8192 matrix.
All inputs are finite; a program needn't handle non-finite values. No bound on the sum of `pinned_cells` on one device may be relied on, other than what follows from the above.
Results may differ from a plain program's by a relative error of at most 0.0003.
Values sent between devices are 32-bit elements; how exact they have to be, the bound alone decides.
No kernel may reach another device: no remote copies, remote signals or barrier semaphores. Data moves between devices by JAX's collectives and lax.ppermute only.
A program may use at most 128 MiB of HBM per device.

v0:
```python
import jax
import jax.numpy as jnp
from jax import lax
from jax.experimental import pallas as pl
from jax.experimental.pallas import tpu as pltpu
from jax.sharding import Mesh
from jax.sharding import PartitionSpec as P

GRP = ("grp_0", "grp_1")
SUB = ("sub_0", "sub_1", "sub_2")
N_GRP, N_SUB = 8, 32
F32, BF16 = jnp.float32, jnp.bfloat16
HIGHEST = lax.Precision.HIGHEST
CX, CY, CZ, SRC, VEC = 16, 16, 128, 16, 32
FIELD = (SRC, CX, CY, CZ)


def iota(shape, dim):
    return lax.broadcasted_iota(jnp.int32, shape, dim)


def exact_dot(left, right):
    return jnp.dot(left, right, precision=HIGHEST, preferred_element_type=F32)


def split(value):
    high = value.astype(BF16)
    return high, (value - high.astype(F32)).astype(BF16)


def dot3(left, right, dims):
    (lh, ll), (rh, rl) = left, right

    def one(a, b):
        return lax.dot_general(a, b, (dims, ((), ())), preferred_element_type=F32)

    return one(lh, rh) + (one(lh, rl) + one(ll, rh))


ROWS_BY_ROWS = ((1,), (1,))
PLAIN = ((1,), (0,))


def slab(ref, x):
    count = ref.shape[0]
    halves = [ref[:, x, 8 * h : 8 * h + 8, :].reshape(count * 8, CZ) for h in range(2)]
    return jnp.concatenate(halves, axis=1)


def pack(total):
    rows = total.shape[0]
    same = iota(total.shape, 0) % 8 == iota(total.shape, 1) % 8
    summed = jnp.where(same, total, 0.0).reshape(rows // 8, 8, 128).sum(axis=1)
    spread = exact_dot(summed, (iota((128, 128), 0) // 8 == iota((128, 128), 1) % 16).astype(F32))
    mine = iota(spread.shape, 0) % 8 == iota(spread.shape, 1) // 16
    return jnp.where(mine, spread, 0.0).reshape(rows // 64, 8, 128).sum(axis=1)


def spread_rows(packed):
    count = packed.shape[0]
    pieces = [jnp.broadcast_to(packed[r : r + 1], (8, 128)) for r in range(count)]
    wide = jnp.concatenate(pieces, axis=0)
    return jnp.where(iota(wide.shape, 0) % 8 == iota(wide.shape, 1) // 16, wide, 0.0)


def unpack(packed, offset):
    pick = iota((128, 128), 0) % 16 == iota((128, 128), 1) - offset
    return exact_dot(spread_rows(packed), pick.astype(F32))


def kron_rows(values):
    count = values.shape[0]
    pieces = [jnp.broadcast_to(values[n : n + 1], (8, 128)) for n in range(count)]
    wide = jnp.concatenate(pieces, axis=0)
    return jnp.where(iota(wide.shape, 0) % 8 == iota(wide.shape, 1) % 8, wide, 0.0)


def put_copies(out_ref, value):
    for n in range(out_ref.shape[0]):
        out_ref[n] = value


def add_up(ref):
    total = ref[0]
    for n in range(1, ref.shape[0]):
        total = total + ref[n]
    return total


def faces_kernel(cond, pinned, x_lo, x_hi, y_lo, y_hi, scaling, keep, coef):
    g = lax.axis_index("grp_0") * 4 + lax.axis_index("grp_1")
    s = (lax.axis_index("sub_0") * 4 + lax.axis_index("sub_1")) * 2 + lax.axis_index("sub_2")

    def inside(count, flag):
        return jnp.broadcast_to(flag.astype(F32), (count, CZ))

    has_x_lo, has_x_hi = inside(CY, g > 0), inside(CY, g < N_GRP - 1)
    has_y_lo, has_y_hi = inside(1, s > 0), inside(1, s < N_SUB - 1)
    rows = iota((CY, CZ), 0)
    lanes = iota((CY, CZ), 1)

    def down(v, edge):
        return jnp.where(rows == 0, edge, pltpu.roll(v, 1, 0))

    def up(v, edge):
        return jnp.where(rows == CY - 1, edge, pltpu.roll(v, CY - 1, 0))

    def left(v):
        return jnp.where(lanes == 0, 0.0, pltpu.roll(v, 1, 1))

    def right(v):
        return jnp.where(lanes == CZ - 1, 0.0, pltpu.roll(v, CZ - 1, 1))

    for x in range(CX):
        keep[x] = 1.0 - pinned[x].astype(F32)
    for x in range(CX):
        c, k = cond[x], keep[x]
        c_lo = cond[x - 1] if x else has_x_lo * x_lo[...]
        c_hi = cond[x + 1] if x < CX - 1 else has_x_hi * x_hi[...]
        k_lo = keep[x - 1] if x else has_x_lo
        k_hi = keep[x + 1] if x < CX - 1 else has_x_hi
        beside = [
            (c_lo, k_lo),
            (c_hi, k_hi),
            (down(c, has_y_lo * y_lo[x : x + 1]), down(k, has_y_lo)),
            (up(c, has_y_hi * y_hi[x : x + 1]), up(k, has_y_hi)),
            (left(c), left(k)),
            (right(c), right(k)),
        ]
        centre = None
        for n, (other, mask) in enumerate(beside):
            face = 0.5 * (c + other)
            centre = face if centre is None else centre + face
            coef[n, x] = (k * mask) * face
        whole = k * centre + (1.0 - k)
        coef[6, x] = whole
        scaling[x] = 1.0 / whole


def restrict_kernel(basis, field, out, total):
    total[...] = jnp.zeros_like(total)

    def step(x, carry):
        total[...] += dot3(split(slab(basis, x)), split(slab(field, x)), ROWS_BY_ROWS)
        return carry

    lax.fori_loop(0, CX, step, 0)
    packed = jnp.concatenate([pack(total[...]), jnp.zeros((4, 128), F32)], axis=0)
    put_copies(out, packed)


def coarse_kernel(gathered, inverse, out, wide):
    for s in range(N_SUB):
        wide[32 * s : 32 * s + 32] = spread_rows(gathered[s, 0:4])
    rows = inverse[...].reshape(N_GRP * VEC, N_SUB * VEC)
    partial = dot3(split(rows), split(wide[...]), PLAIN)
    merge = (iota((128, 128), 0) % 16 == iota((128, 128), 1) % 16).astype(F32)
    partial = exact_dot(partial, merge)
    mine = iota(partial.shape, 0) % 8 == iota(partial.shape, 1) // 16
    partial = jnp.where(mine, partial, 0.0).reshape(N_GRP * 4, 8, 128).sum(axis=1)
    carried = add_up(gathered)[4:8]
    for g in range(N_GRP):
        out[g] = jnp.concatenate([partial[4 * g : 4 * g + 4], carried], axis=0)


def prolong_kernel(arrived, basis, field, scaling, keep, out, x_lo, x_hi, y_lo, y_hi, carried):
    total = add_up(arrived)
    carried[...] = total
    pick = iota((128, 128), 0) % 16 == iota((128, 128), 1) // 8
    values = exact_dot(spread_rows(total[0:4]), pick.astype(F32))
    matrix = split(kron_rows(values).T)

    def step(x, carry):
        product = dot3(matrix, split(slab(basis, x)), PLAIN)
        for h in range(2):
            cells = pl.ds(8 * h, 8)
            coarse = product[:, CZ * h : CZ * h + CZ].reshape(SRC, 8, CZ)
            out[:, x, cells, :] = scaling[x, cells, :] * field[:, x, cells, :] + coarse
        y_lo[:, pl.ds(x, 1), :] = keep[x, 0:1, :] * out[:, x, 0:1, :]
        y_hi[:, pl.ds(x, 1), :] = keep[x, 15:16, :] * out[:, x, 15:16, :]
        return carry

    lax.fori_loop(0, CX, step, 0)
    x_lo[...] = keep[0] * out[:, 0]
    x_hi[...] = keep[CX - 1] * out[:, CX - 1]


def stencil(x, j, field, x_lo, x_hi, y_lo, y_hi, coef, edge):
    rows = iota((CY, CZ), 0)
    v = field[j, x]
    if edge == 0:
        low, high = x_lo[j], field[j, x + 1]
    elif edge == 1:
        low, high = field[j, x - 1], x_hi[j]
    else:
        low, high = field[j, x - 1], field[j, x + 1]
    down = jnp.where(rows == 0, y_lo[j, pl.ds(x, 1), :], pltpu.roll(v, 1, 0))
    up = jnp.where(rows == CY - 1, y_hi[j, pl.ds(x, 1), :], pltpu.roll(v, CY - 1, 0))
    left, right = pltpu.roll(v, 1, 1), pltpu.roll(v, CZ - 1, 1)
    beside = coef[0, x] * low + coef[1, x] * high
    beside = beside + coef[2, x] * down + coef[3, x] * up
    beside = beside + coef[4, x] * left + coef[5, x] * right
    return coef[6, x] * v - beside


def apply_everywhere(field, x_lo, x_hi, y_lo, y_hi, coef, image):
    def plane(x, edge):
        for j in range(SRC):
            image[j, x] = stencil(x, j, field, x_lo, x_hi, y_lo, y_hi, coef, edge)

    def middle(x, carry):
        plane(x, 2)
        return carry

    plane(0, 0)
    lax.fori_loop(1, CX - 1, middle, 0)
    plane(CX - 1, 1)


def first_image_kernel(
    field, x_lo, x_hi, y_lo, y_hi, coef, basis, right_side, image, out, total, gram_a, gram_b
):
    apply_everywhere(field, x_lo, x_hi, y_lo, y_hi, coef, image)
    for ref in (total, gram_a, gram_b):
        ref[...] = jnp.zeros_like(ref)

    def step(x, carry):
        applied = split(slab(image, x))
        direction = split(slab(field, x))
        total[...] += dot3(split(slab(basis, x)), applied, ROWS_BY_ROWS)
        gram_a[...] += dot3(direction, split(slab(right_side, x)), ROWS_BY_ROWS)
        gram_b[...] += dot3(direction, applied, ROWS_BY_ROWS)
        return carry

    lax.fori_loop(0, CX, step, 0)
    packed = [pack(total[...]), pack(gram_a[...]), pack(gram_b[...])]
    put_copies(out, jnp.concatenate(packed, axis=0))


def second_image_kernel(
    field, x_lo, x_hi, y_lo, y_hi, coef, first_image, image, out, gram_c, gram_d
):
    apply_everywhere(field, x_lo, x_hi, y_lo, y_hi, coef, image)
    for ref in (gram_c, gram_d):
        ref[...] = jnp.zeros_like(ref)

    def step(x, carry):
        second = split(slab(field, x))
        gram_c[...] += dot3(split(slab(first_image, x)), second, ROWS_BY_ROWS)
        gram_d[...] += dot3(split(slab(image, x)), second, ROWS_BY_ROWS)
        return carry

    lax.fori_loop(0, CX, step, 0)
    cross = gram_c[...]
    packed = [pack(cross), pack(cross.T), pack(gram_d[...]), jnp.zeros((2, 128), F32)]
    put_copies(out, jnp.concatenate(packed, axis=0))


def relay_kernel(arrived, out):
    put_copies(out, add_up(arrived))


def eliminate(matrix):
    rows = iota(matrix.shape, 0)
    for p in range(16):
        row = matrix[p : p + 1] / matrix[p : p + 1, p : p + 1]
        column = matrix[:, p : p + 1]
        matrix = jnp.where(rows == p, row, matrix - column * row)
    return matrix


def tall(matrix):
    return jnp.concatenate([matrix, jnp.zeros((112, 128), F32)], axis=0)


def finish_kernel(
    arrived, carried, first, second, first_image, second_image, right_side, solution, residual
):
    total = add_up(arrived)
    cross, crossed, energy = total[0:2], total[2:4], total[4:6]
    projection, curvature = carried[4:6], carried[6:8]
    lanes = iota((16, 128), 1)
    solved = eliminate(unpack(curvature, 0) + unpack(projection, 16) + unpack(cross, 32))
    back = exact_dot(unpack(crossed, 0), tall(solved))
    reduced = unpack(energy, 0) - pltpu.roll(back, 96, 1)
    target = back - unpack(curvature, 16)
    last = eliminate(jnp.where(lanes < 16, reduced, jnp.where(lanes < 32, target, 0.0)))
    mix = jnp.where(lanes < 16, pltpu.roll(solved, 96, 1), 0.0)
    on_first = solved + exact_dot(mix, tall(last))
    pick = (iota((128, 128), 0) - 16 == iota((128, 128), 1) // 8).astype(F32)
    on_first = kron_rows(exact_dot(on_first, pick))
    on_second = kron_rows(exact_dot(-last, pick))
    matrix = split(jnp.concatenate([on_first, on_second], axis=0).T)

    def step(x, carry):
        pair = jnp.concatenate([slab(first, x), slab(second, x)], axis=0)
        images = jnp.concatenate([slab(first_image, x), slab(second_image, x)], axis=0)
        moved = dot3(matrix, split(pair), PLAIN)
        removed = dot3(matrix, split(images), PLAIN)
        for h in range(2):
            cells = pl.ds(8 * h, 8)
            part = slice(CZ * h, CZ * h + CZ)
            solution[:, x, cells, :] = moved[:, part].reshape(SRC, 8, CZ)
            residual[:, x, cells, :] = right_side[:, x, cells, :] - removed[:, part].reshape(
                SRC, 8, CZ
            )
        return carry

    lax.fori_loop(0, CX, step, 0)


INTERPRET = False


def call(kernel, out_shapes, scratch, *args):
    return pl.pallas_call(
        kernel,
        out_shape=[jax.ShapeDtypeStruct(s, F32) for s in out_shapes],
        in_specs=[pl.BlockSpec(memory_space=pltpu.VMEM)] * len(args),
        out_specs=[pl.BlockSpec(memory_space=pltpu.VMEM)] * len(out_shapes),
        scratch_shapes=[pltpu.VMEM(s, F32) for s in scratch],
        compiler_params=pltpu.CompilerParams(vmem_limit_bytes=48 * 1024 * 1024),
        interpret=INTERPRET,
    )(*args)


def exchange(pieces, axes):
    return lax.all_to_all(pieces, axes, split_axis=0, concat_axis=0, tiled=True)


def swap_edges(low, high, axes):
    count = lax.axis_size(axes)
    up = [(i, (i + 1) % count) for i in range(count)]
    return lax.ppermute(high, axes, up), lax.ppermute(low, axes, [(b, a) for a, b in up])


def local(right_side, conductivity, pinned_cells, coarse_basis, coarse_inverse):
    face = (SRC, CY, CZ)
    block = (CX, CY, CZ)
    tile = (8, 128)

    def coarse_answer(pieces):
        gathered = exchange(pieces, SUB)
        (partial,) = call(
            coarse_kernel, [(N_GRP, *tile)], [(N_SUB * VEC, 128)], gathered, coarse_inverse
        )
        return exchange(partial, GRP)

    def precondition(pieces, field):
        out = call(
            prolong_kernel,
            [FIELD, face, face, face, face, tile],
            [],
            coarse_answer(pieces),
            coarse_basis,
            field,
            scaling,
            keep,
        )
        smoothed, x_lo, x_hi, y_lo, y_hi, carried = out
        edges = (*swap_edges(x_lo, x_hi, GRP), *swap_edges(y_lo, y_hi, SUB))
        return smoothed, edges, carried

    x_edges = swap_edges(conductivity[0], conductivity[-1], GRP)
    y_edges = swap_edges(conductivity[:, 0], conductivity[:, -1], SUB)
    (pieces,) = call(
        restrict_kernel, [(N_SUB, *tile)], [(VEC * 8, 128)], coarse_basis, right_side
    )
    scaling, keep, coef = call(
        faces_kernel,
        [block, block, (7, *block)],
        [],
        conductivity,
        pinned_cells,
        *x_edges,
        *y_edges,
    )
    first, edges, _ = precondition(pieces, right_side)
    first_image, pieces = call(
        first_image_kernel,
        [FIELD, (N_SUB, *tile)],
        [(VEC * 8, 128), (128, 128), (128, 128)],
        first,
        *edges,
        coef,
        coarse_basis,
        right_side,
    )
    second, edges, carried = precondition(pieces, first_image)
    second_image, pieces = call(
        second_image_kernel,
        [FIELD, (N_GRP, *tile)],
        [(128, 128), (128, 128)],
        second,
        *edges,
        coef,
        first_image,
    )
    (pieces,) = call(relay_kernel, [(N_SUB, *tile)], [], exchange(pieces, GRP))
    return tuple(
        call(
            finish_kernel,
            [FIELD, FIELD],
            [],
            exchange(pieces, SUB),
            carried,
            first,
            second,
            first_image,
            second_image,
            right_side,
        )
    )


def solution(mesh):
    split_mesh = Mesh(
        mesh.devices.reshape(2, 4, 4, 4, 2), ("grp_0", "grp_1", "sub_0", "sub_1", "sub_2")
    )
    in_specs = (
        P(None, GRP, SUB, None),
        P(GRP, SUB, None),
        P(GRP, SUB, None),
        P(None, GRP, SUB, None),
        P(None, SUB, GRP),
    )
    out_specs = (P(None, GRP, SUB, None), P(None, GRP, SUB, None))
    return jax.shard_map(
        local, mesh=split_mesh, in_specs=in_specs, out_specs=out_specs, check_vma=False
    )
```

profile of v0, /device:TPU:1, one launch (start us, length us, event | category | flops | bytes accessed | tf_op | source)
XLA Modules:
  0.0 180.3 jit_solution(14296925917108411641)
XLA Ops:
  0.6 0.0 copy-start
  0.6 1.6 copy-done
  2.2 0.0 copy-start.7
  2.2 0.0 copy-start.3
  2.2 0.0 copy-start.1
  2.2 7.5 %shard_map.68 = f32[32,8,128]{2,1,0:T(8,128)} custom-call(f32[32,16,16,128]{3,2,1,0:T(8,128)} %basis.7, f32[16,16,16,128]{3,2,1,0:T(8,128)S(1)} %copy-done), custom_call_target="tpu_custom_call" | custom-call | tf_op jit(solution)/shard_map/pallas_call | solution.py:316
  9.8 12.6 %all-to-all-start = ((f32[32,8,128]{2,1,0:T(8,128)}), f32[32,8,128]{2,1,0:T(8,128)S(1)}, u32[]{:S(2)}, u32[]{:S(2)}) async-start(f32[32,8,128]{2,1,0:T(8,128)} %shard_map.68), calls=%async_computation | async-start | bytes 262144 | tf_op jit(solution)/shard_map/all_to_all | solution.py:328
  22.3 0.0 copy-done.7
  22.4 1.7 collective-permute-start.2
  24.1 0.0 collective-permute-start.3
  24.1 9.2 %all-to-all-done.gathered = f32[32,8,128]{2,1,0:T(8,128)S(1)} async-done(((f32[32,8,128]{2,1,0:T(8,128)}), f32[32,8,128]{2,1,0:T(8,128)S(1)}, u32[]{:S(2)}, u32[]{:S(2)}) %all-to-all-start) | async-done | bytes 131104 | tf_op jit(solution)/shard_map/all_to_all | solution.py:328
  33.3 0.0 copy-done.3
  33.3 1.6 shard_map.69
  34.9 4.5 %all-to-all-start.1 = ((f32[8,8,128]{2,1,0:T(8,128)}), f32[8,8,128]{2,1,0:T(8,128)}, u32[]{:S(2)}, u32[]{:S(2)}) async-start(f32[8,8,128]{2,1,0:T(8,128)} %shard_map.69), calls=%async_computation.1 | async-start | bytes 65536 | tf_op jit(solution)/shard_map/all_to_all | solution.py:328
  39.4 3.6 %collective-permute-start.1 = (f32[16,128]{1,0:T(8,128)S(1)}, f32[16,128]{1,0:T(8,128)S(1)}, u32[]{:S(2)}, u32[]{:S(2)}) collective-permute-start(f32[16,128]{1,0:T(8,128)S(1)} %get-tuple-element.40), channel_id=1, source_target_pairs={{32,0},{64,32},{96,64},{128,96},{160,128},{192,160},{224,192},{0,2... | collective-permute-start | bytes 24584 | tf_op jit(solution)/shard_map/ppermute | solution.py:334
  43.0 0.0 collective-permute-start
  43.0 0.0 collective-permute-done.2.y_lo
  43.0 0.0 collective-permute-done.3.y_hi
  43.0 0.8 collective-permute-done.1.x_hi
  43.8 3.8 %collective-permute-done.x_lo = f32[16,128]{1,0:T(8,128)S(1)} collective-permute-done((f32[16,128]{1,0:T(8,128)S(1)}, f32[16,128]{1,0:T(8,128)S(1)}, u32[]{:S(2)}, u32[]{:S(2)}) %collective-permute-start) | collective-permute-done | bytes 8224 | tf_op jit(solution)/shard_map/ppermute | solution.py:334
  47.6 0.0 copy-start.8
  47.6 0.9 copy-done.8
  48.5 0.2 shard_map.70
  48.7 0.0 copy-start.4
  48.8 0.9 copy-done.4
  49.7 0.0 all-to-all-done.1.arrived
  49.7 0.0 copy-done.1
  49.7 0.0 copy-start.5
  49.7 7.0 %shard_map.71 = (f32[16,16,16,128]{3,2,1,0:T(8,128)S(1)}, f32[16,16,128]{2,1,0:T(8,128)S(1)}, f32[16,16,128]{2,1,0:T(8,128)S(1)}, f32[16,16,128]{2,1,0:T(8,128)S...) custom-call(f32[8,8,128]{2,1,0:T(8,128)} %all-to-all-done.1.arrived, f32[32,16,16,128]{3,2,1,0:T(8,128)} %basis.7, ...), custom_call_target="tpu_custom_call" | custom-call | tf_op jit(solution)/shard_map/pallas_call | solution.py:316
  56.6 0.0 collective-permute-start.4
  56.6 3.6 %collective-permute-start.5 = (f32[16,16,128]{2,1,0:T(8,128)S(1)}, f32[16,16,128]{2,1,0:T(8,128)S(1)}, u32[]{:S(2)}, u32[]{:S(2)}) collective-permute-start(f32[16,16,128]{2,1,0:T(8,128)S(1)} %get-tuple-element.24), channel_id=1, source_target_pairs={{32,0},{64,32},{96,64},{128,96},{160,128},{192,160},{224,192},{0,2... | collective-permute-start | bytes 393224 | tf_op jit(solution)/shard_map/ppermute | solution.py:334
  60.2 2.7 %collective-permute-start.6 = (f32[16,16,128]{2,1,0:T(8,128)S(1)}, f32[16,16,128]{2,1,0:T(8,128)S(1)}, u32[]{:S(2)}, u32[]{:S(2)}) collective-permute-start(f32[16,16,128]{2,1,0:T(8,128)S(1)} %get-tuple-element.25), channel_id=1, source_target_pairs={{0,1},{1,2},{2,3},{3,4},{4,5},{5,6},{6,7},{7,8},{8,9},{9,10},{10,1... | collective-permute-start | bytes 393224 | tf_op jit(solution)/shard_map/ppermute | solution.py:334
  63.0 0.1 collective-permute-start.7
  63.1 0.0 collective-permute-done.4.x_lo
  63.1 0.0 collective-permute-done.5.x_hi
  63.1 1.8 %collective-permute-done.6.y_lo = f32[16,16,128]{2,1,0:T(8,128)S(1)} collective-permute-done((f32[16,16,128]{2,1,0:T(8,128)S(1)}, f32[16,16,128]{2,1,0:T(8,128)S(1)}, u32[]{:S(2)}, u32[]{:S(2)}) %collective-permute-start.6) | collective-permute-done | bytes 131104 | tf_op jit(solution)/shard_map/ppermute | solution.py:334
  64.9 2.4 %collective-permute-done.7.y_hi = f32[16,16,128]{2,1,0:T(8,128)S(1)} collective-permute-done((f32[16,16,128]{2,1,0:T(8,128)S(1)}, f32[16,16,128]{2,1,0:T(8,128)S(1)}, u32[]{:S(2)}, u32[]{:S(2)}) %collective-permute-start.7) | collective-permute-done | bytes 131104 | tf_op jit(solution)/shard_map/ppermute | solution.py:334
  67.4 0.0 copy-done.5
  67.4 11.6 %shard_map.72 = (f32[16,16,16,128]{3,2,1,0:T(8,128)S(1)}, f32[32,8,128]{2,1,0:T(8,128)S(1)}) custom-call(f32[16,16,16,128]{3,2,1,0:T(8,128)S(1)} %get-tuple-element.22.field.first, f32[16,16,128]{2,1,0:T(8,128)S(1)} %collective-permute-done.4.x_lo, f32[16,16,128]{2,1,0:T(8,128)S(1)} %collective-permute-done.5.x_hi, ...), custom_call_target="tpu_custom_call" | custom-call | tf_op jit(solution)/shard_map/pallas_call | solution.py:316
  79.0 0.0 copy-start.2
  79.0 23.3 %all_to_all.30.gathered = f32[32,8,128]{2,1,0:T(8,128)S(1)} all-to-all(f32[32,8,128]{2,1,0:T(8,128)S(1)} %get-tuple-element.28), channel_id=1, replica_groups=mesh['grp_0'=2,'grp_1'=4,'sub_0'=4,'sub_1'=4,'sub_2'=2] {'sub_0','sub_1'..., dimensions={0} | all-to-all | bytes 262144 | tf_op jit(solution)/shard_map/all_to_all | solution.py:328
  102.3 1.0 shard_map.73
  103.3 7.5 %all_to_all.31.arrived = f32[8,8,128]{2,1,0:T(8,128)S(1)} all-to-all(f32[8,8,128]{2,1,0:T(8,128)S(1)} %shard_map.73), channel_id=1, replica_groups=mesh['grp_0'=2,'grp_1'=4,'sub_0'=4,'sub_1'=4,'sub_2'=2] {'grp_0','grp_1'}, dimensions={0} | all-to-all | bytes 65536 | tf_op jit(solution)/shard_map/all_to_all | solution.py:328
  110.8 6.3 %shard_map.74 = (f32[16,16,16,128]{3,2,1,0:T(8,128)S(1)}, f32[16,16,128]{2,1,0:T(8,128)S(1)}, f32[16,16,128]{2,1,0:T(8,128)S(1)}, f32[16,16,128]{2,1,0:T(8,128)S...) custom-call(f32[8,8,128]{2,1,0:T(8,128)S(1)} %all_to_all.31.arrived, f32[32,16,16,128]{3,2,1,0:T(8,128)} %basis.7, ...), custom_call_target="tpu_custom_call" | custom-call | tf_op jit(solution)/shard_map/pallas_call | solution.py:316
  117.1 0.0 copy-done.2
  117.1 0.4 collective-permute-start.8
  117.5 3.3 %collective-permute-start.9 = (f32[16,16,128]{2,1,0:T(8,128)S(1)}, f32[16,16,128]{2,1,0:T(8,128)S(1)}, u32[]{:S(2)}, u32[]{:S(2)}) collective-permute-start(f32[16,16,128]{2,1,0:T(8,128)S(1)} %get-tuple-element.32), channel_id=1, source_target_pairs={{32,0},{64,32},{96,64},{128,96},{160,128},{192,160},{224,192},{0,2... | collective-permute-start | bytes 393224 | tf_op jit(solution)/shard_map/ppermute | solution.py:334
  120.8 1.7 collective-permute-start.10
  122.4 0.2 collective-permute-start.11
  122.6 0.5 collective-permute-done.8.x_lo
  123.1 0.0 collective-permute-done.9.x_hi
  123.1 1.3 collective-permute-done.10.y_lo
  124.4 2.4 %collective-permute-done.11.y_hi = f32[16,16,128]{2,1,0:T(8,128)S(1)} collective-permute-done((f32[16,16,128]{2,1,0:T(8,128)S(1)}, f32[16,16,128]{2,1,0:T(8,128)S(1)}, u32[]{:S(2)}, u32[]{:S(2)}) %collective-permute-start.11) | collective-permute-done | bytes 131104 | tf_op jit(solution)/shard_map/ppermute | solution.py:334
  126.8 8.6 %shard_map.75 = (f32[16,16,16,128]{3,2,1,0:T(8,128)S(1)}, f32[8,8,128]{2,1,0:T(8,128)S(1)}) custom-call(f32[16,16,16,128]{3,2,1,0:T(8,128)S(1)} %get-tuple-element.30.field.second, f32[16,16,128]{2,1,0:T(8,128)S(1)} %collective-permute-done.8.x_lo, f32[16,16,128]{2,1,0:T(8,128)S(1)} %collective-permute-done.9.x_hi, ...), custom_call_target="tpu_custom_call" | custom-call | tf_op jit(solution)/shard_map/pallas_call | solution.py:316
  135.5 0.0 copy-start.6
  135.5 1.3 copy-done.6
  136.8 7.5 %all_to_all.32.arrived = f32[8,8,128]{2,1,0:T(8,128)S(1)} all-to-all(f32[8,8,128]{2,1,0:T(8,128)S(1)} %get-tuple-element.35), channel_id=1, replica_groups=mesh['grp_0'=2,'grp_1'=4,'sub_0'=4,'sub_1'=4,'sub_2'=2] {'grp_0','grp_1'}, dimensions={0} | all-to-all | bytes 65536 | tf_op jit(solution)/shard_map/all_to_all | solution.py:328
  144.3 22.7 %all_to_all.33.arrived = f32[32,8,128]{2,1,0:T(8,128)S(1)} all-to-all(f32[32,8,128]{2,1,0:T(8,128)S(1)} %shard_map.76), channel_id=1, replica_groups=mesh['grp_0'=2,'grp_1'=4,'sub_0'=4,'sub_1'=4,'sub_2'=2] {'sub_0','sub_1'..., dimensions={0} | all-to-all | bytes 262144 | tf_op jit(solution)/shard_map/all_to_all | solution.py:328
  166.9 13.4 %shard_map.77 = (f32[16,16,16,128]{3,2,1,0:T(8,128)}, f32[16,16,16,128]{3,2,1,0:T(8,128)}) custom-call(f32[32,8,128]{2,1,0:T(8,128)S(1)} %all_to_all.33.arrived, f32[8,128]{1,0:T(8,128)S(1)} %get-tuple-element.36.carried, f32[16,16,16,128]{3,2,1,0:T(8,128)S(1)} %get-tuple-element.22.field.first, f32[16,16,16,128]{3,2,1,0:T(8,128)S(1)} %get-tuple-element.30.field.second, ...), custom_call_target="tpu_custom_call" | custom-call | tf_op jit(solution)/shard_map/pallas_call | solution.py:316
  (3 shorter events, 0.0 us)
Async XLA Ops:
  0.6 1.6 copy-start
  2.2 20.1 %copy-start.7 = (f32[16,16,128]{2,1,0:T(8,128)S(1)}, f32[16,16,128]{2,1,0:T(8,128)}, u32[]{:S(2)}) copy-start(f32[16,16,128]{2,1,0:T(8,128)} %cond.1) | copy-start | bytes 393220
  2.2 31.1 %copy-start.3 = (f32[8,32,1024]{2,1,0:T(8,128)S(1)}, f32[8,32,1024]{2,1,0:T(8,128)}, u32[]{:S(2)}) copy-start(f32[8,32,1024]{2,1,0:T(8,128)} %inverse.3) | copy-start | bytes 3145732
  2.2 47.5 %copy-start.1 = (f32[16,16,16,128]{3,2,1,0:T(8,128)S(1)}, f32[16,16,16,128]{3,2,1,0:T(8,128)}, u32[]{:S(2)}) copy-start(f32[16,16,16,128]{3,2,1,0:T(8,128)} %right_side.3) | copy-start | bytes 6291460
  9.8 23.5 %all-to-all-start = ((f32[32,8,128]{2,1,0:T(8,128)}), f32[32,8,128]{2,1,0:T(8,128)S(1)}, u32[]{:S(2)}, u32[]{:S(2)}) async-start(f32[32,8,128]{2,1,0:T(8,128)} %shard_map.68), calls=%async_computation | async-start | bytes 262144 | tf_op jit(solution)/shard_map/all_to_all | solution.py:328
  22.4 20.6 %collective-permute-start.2 = (f32[16,128]{1,0:T(8,128)S(1)}, f32[16,128]{1,0:T(8,128)S(1)}, u32[]{:S(2)}, u32[]{:S(2)}) collective-permute-start(f32[16,128]{1,0:T(8,128)S(1)} %bitcast.11), channel_id=1, source_target_pairs={{0,1},{1,2},{2,3},{3,4},{4,5},{5,6},{6,7},{7,8},{8,9},{9,10},{10,1... | collective-permute-start | bytes 24584 | tf_op jit(solution)/shard_map/ppermute | solution.py:334
  24.1 18.9 %collective-permute-start.3 = (f32[16,128]{1,0:T(8,128)S(1)}, f32[16,128]{1,0:T(8,128)S(1)}, u32[]{:S(2)}, u32[]{:S(2)}) collective-permute-start(f32[16,128]{1,0:T(8,128)S(1)} %bitcast.10), channel_id=1, source_target_pairs={{1,0},{2,1},{3,2},{4,3},{5,4},{6,5},{7,6},{8,7},{9,8},{10,9},{11,1... | collective-permute-start | bytes 24584 | tf_op jit(solution)/shard_map/ppermute | solution.py:334
  34.9 14.8 %all-to-all-start.1 = ((f32[8,8,128]{2,1,0:T(8,128)}), f32[8,8,128]{2,1,0:T(8,128)}, u32[]{:S(2)}, u32[]{:S(2)}) async-start(f32[8,8,128]{2,1,0:T(8,128)} %shard_map.69), calls=%async_computation.1 | async-start | bytes 65536 | tf_op jit(solution)/shard_map/all_to_all | solution.py:328
  39.4 4.4 %collective-permute-start.1 = (f32[16,128]{1,0:T(8,128)S(1)}, f32[16,128]{1,0:T(8,128)S(1)}, u32[]{:S(2)}, u32[]{:S(2)}) collective-permute-start(f32[16,128]{1,0:T(8,128)S(1)} %get-tuple-element.40), channel_id=1, source_target_pairs={{32,0},{64,32},{96,64},{128,96},{160,128},{192,160},{224,192},{0,2... | collective-permute-start | bytes 24584 | tf_op jit(solution)/shard_map/ppermute | solution.py:334
  43.0 4.6 %collective-permute-start = (f32[16,128]{1,0:T(8,128)S(1)}, f32[16,128]{1,0:T(8,128)S(1)}, u32[]{:S(2)}, u32[]{:S(2)}) collective-permute-start(f32[16,128]{1,0:T(8,128)S(1)} %get-tuple-element.41), channel_id=1, source_target_pairs={{0,32},{32,64},{64,96},{96,128},{128,160},{160,192},{192,224},{224... | collective-permute-start | bytes 24584 | tf_op jit(solution)/shard_map/ppermute | solution.py:334
  47.6 0.9 copy-start.8
  48.7 0.9 copy-start.4
  49.7 17.7 %copy-start.5 = (f32[7,16,16,128]{3,2,1,0:T(8,128)S(1)}, f32[7,16,16,128]{3,2,1,0:T(8,128)}, u32[]{:S(2)}) copy-start(f32[7,16,16,128]{3,2,1,0:T(8,128)} %copy-done.4) | copy-start | bytes 2752516
  56.6 6.4 %collective-permute-start.4 = (f32[16,16,128]{2,1,0:T(8,128)S(1)}, f32[16,16,128]{2,1,0:T(8,128)S(1)}, u32[]{:S(2)}, u32[]{:S(2)}) collective-permute-start(f32[16,16,128]{2,1,0:T(8,128)S(1)} %get-tuple-element.23), channel_id=1, source_target_pairs={{0,32},{32,64},{64,96},{96,128},{128,160},{160,192},{192,224},{224... | collective-permute-start | bytes 393224 | tf_op jit(solution)/shard_map/ppermute | solution.py:334
  56.6 6.4 %collective-permute-start.5 = (f32[16,16,128]{2,1,0:T(8,128)S(1)}, f32[16,16,128]{2,1,0:T(8,128)S(1)}, u32[]{:S(2)}, u32[]{:S(2)}) collective-permute-start(f32[16,16,128]{2,1,0:T(8,128)S(1)} %get-tuple-element.24), channel_id=1, source_target_pairs={{32,0},{64,32},{96,64},{128,96},{160,128},{192,160},{224,192},{0,2... | collective-permute-start | bytes 393224 | tf_op jit(solution)/shard_map/ppermute | solution.py:334
  60.2 4.7 %collective-permute-start.6 = (f32[16,16,128]{2,1,0:T(8,128)S(1)}, f32[16,16,128]{2,1,0:T(8,128)S(1)}, u32[]{:S(2)}, u32[]{:S(2)}) collective-permute-start(f32[16,16,128]{2,1,0:T(8,128)S(1)} %get-tuple-element.25), channel_id=1, source_target_pairs={{0,1},{1,2},{2,3},{3,4},{4,5},{5,6},{6,7},{7,8},{8,9},{9,10},{10,1... | collective-permute-start | bytes 393224 | tf_op jit(solution)/shard_map/ppermute | solution.py:334
  63.0 4.4 %collective-permute-start.7 = (f32[16,16,128]{2,1,0:T(8,128)S(1)}, f32[16,16,128]{2,1,0:T(8,128)S(1)}, u32[]{:S(2)}, u32[]{:S(2)}) collective-permute-start(f32[16,16,128]{2,1,0:T(8,128)S(1)} %get-tuple-element.26), channel_id=1, source_target_pairs={{1,0},{2,1},{3,2},{4,3},{5,4},{6,5},{7,6},{8,7},{9,8},{10,9},{11,1... | collective-permute-start | bytes 393224 | tf_op jit(solution)/shard_map/ppermute | solution.py:334
  79.0 38.1 %copy-start.2 = (f32[16,16,16,128]{3,2,1,0:T(8,128)}, f32[16,16,16,128]{3,2,1,0:T(8,128)S(1)}, u32[]{:S(2)}) copy-start(f32[16,16,16,128]{3,2,1,0:T(8,128)S(1)} %get-tuple-element.29.field.first_image) | copy-start | bytes 6291460
  117.1 6.0 %collective-permute-start.8 = (f32[16,16,128]{2,1,0:T(8,128)S(1)}, f32[16,16,128]{2,1,0:T(8,128)S(1)}, u32[]{:S(2)}, u32[]{:S(2)}) collective-permute-start(f32[16,16,128]{2,1,0:T(8,128)S(1)} %get-tuple-element.31), channel_id=1, source_target_pairs={{0,32},{32,64},{64,96},{96,128},{128,160},{160,192},{192,224},{224... | collective-permute-start | bytes 393224 | tf_op jit(solution)/shard_map/ppermute | solution.py:334
  117.5 5.6 %collective-permute-start.9 = (f32[16,16,128]{2,1,0:T(8,128)S(1)}, f32[16,16,128]{2,1,0:T(8,128)S(1)}, u32[]{:S(2)}, u32[]{:S(2)}) collective-permute-start(f32[16,16,128]{2,1,0:T(8,128)S(1)} %get-tuple-element.32), channel_id=1, source_target_pairs={{32,0},{64,32},{96,64},{128,96},{160,128},{192,160},{224,192},{0,2... | collective-permute-start | bytes 393224 | tf_op jit(solution)/shard_map/ppermute | solution.py:334
  120.8 3.6 %collective-permute-start.10 = (f32[16,16,128]{2,1,0:T(8,128)S(1)}, f32[16,16,128]{2,1,0:T(8,128)S(1)}, u32[]{:S(2)}, u32[]{:S(2)}) collective-permute-start(f32[16,16,128]{2,1,0:T(8,128)S(1)} %get-tuple-element.33), channel_id=1, source_target_pairs={{0,1},{1,2},{2,3},{3,4},{4,5},{5,6},{6,7},{7,8},{8,9},{9,10},{10,1... | collective-permute-start | bytes 393224 | tf_op jit(solution)/shard_map/ppermute | solution.py:334
  122.4 4.4 %collective-permute-start.11 = (f32[16,16,128]{2,1,0:T(8,128)S(1)}, f32[16,16,128]{2,1,0:T(8,128)S(1)}, u32[]{:S(2)}, u32[]{:S(2)}) collective-permute-start(f32[16,16,128]{2,1,0:T(8,128)S(1)} %get-tuple-element.34), channel_id=1, source_target_pairs={{1,0},{2,1},{3,2},{4,3},{5,4},{6,5},{7,6},{8,7},{9,8},{10,9},{11,1... | collective-permute-start | bytes 393224 | tf_op jit(solution)/shard_map/ppermute | solution.py:334
  135.5 1.3 copy-start.6
where the time goes:
time: 181 us; the launch traced here: 180 us
  blocking collectives  61 us (34%)
  Pallas kernels  57.2 us (32%)
  starting transfers between devices  34.3 us (19%)
  waiting for transfers between devices  22.3 us (12%)
  local copies, waits for them, and re-layouts  4.75 us (3%)
    all_to_all x4, blocking collectives, exchange(): return lax.all_to_all(pieces, axes, split_axis=0, concat_axis=0, tiled=True)  61 us
    pallas_call x10, Pallas kernels, call(): pl.pallas_call(kernel, out_shape=[jax.ShapeDtypeStruct(s, F32) for s in o...  57.2 us
    all_to_all x2, starting transfers between devices, exchange(): return lax.all_to_all(pieces, axes, split_axis=0, concat_axis=0, tiled=True)  17.1 us
    ppermute x6, starting transfers between devices, swap_edges(): lax.ppermute(low, axes, [(b, a) for a, b in up])  10.7 us
    all_to_all x2, waiting for transfers between devices, exchange(): return lax.all_to_all(pieces, axes, split_axis=0, concat_axis=0, tiled=True)  9.23 us
    ppermute x6, waiting for transfers between devices, swap_edges(): lax.ppermute(high, axes, up)  7.39 us
    ppermute x6, starting transfers between devices, swap_edges(): lax.ppermute(high, axes, up)  6.53 us
    ppermute x6, waiting for transfers between devices, swap_edges(): lax.ppermute(low, axes, [(b, a) for a, b in up])  5.68 us
  transfers between devices with their start and end apart: 14, of which 8 were waited for; matrix products, arithmetic and copies ran while one was open for 0% of the time, Pallas kernels for 1%

commit v1 on v0

v1 whole, which is shorter than its diff:
```python
import jax
import jax.numpy as jnp
from jax import lax
from jax.experimental import pallas as pl
from jax.experimental.pallas import tpu as pltpu
from jax.sharding import Mesh
from jax.sharding import PartitionSpec as P

GRP = ("grp_0", "grp_1")
SUB = ("sub_0", "sub_1", "sub_2")
N_GRP, N_SUB = 8, 32
F32, BF16 = jnp.float32, jnp.bfloat16
HIGHEST = lax.Precision.HIGHEST
CX, CY, CZ, SRC, VEC = 16, 16, 128, 16, 32
FIELD = (SRC, CX, CY, CZ)


def iota(shape, dim):
    return lax.broadcasted_iota(jnp.int32, shape, dim)


def exact_dot(left, right):
    return jnp.dot(left, right, precision=HIGHEST, preferred_element_type=F32)


def split(value):
    high = value.astype(BF16)
    return high, (value - high.astype(F32)).astype(BF16)


def dot3(left, right, by_rows):
    (lh, ll), (rh, rl) = left, right
    dim = 1 if by_rows else 0
    wide = jnp.concatenate([lh, lh, ll], axis=1)
    deep = jnp.concatenate([rh, rl, rh], axis=dim)
    return lax.dot_general(wide, deep, (((1,), (dim,)), ((), ())), preferred_element_type=F32)


def slab(ref, x):
    count = ref.shape[0]
    halves = [ref[:, x, 8 * h : 8 * h + 8, :].reshape(count * 8, CZ) for h in range(2)]
    return jnp.concatenate(halves, axis=1)


def rows_of(*pairs):
    return tuple(jnp.concatenate(parts, axis=0) for parts in zip(*pairs))


def pack(total):
    rows = total.shape[0]
    same = iota(total.shape, 0) % 8 == iota(total.shape, 1) % 8
    summed = jnp.where(same, total, 0.0).reshape(rows // 8, 8, 128).sum(axis=1)
    spread = exact_dot(summed, (iota((128, 128), 0) // 8 == iota((128, 128), 1) % 16).astype(F32))
    mine = iota(spread.shape, 0) % 8 == iota(spread.shape, 1) // 16
    return jnp.where(mine, spread, 0.0).reshape(rows // 64, 8, 128).sum(axis=1)


def spread_rows(packed):
    count = packed.shape[0]
    pieces = [jnp.broadcast_to(packed[r : r + 1], (8, 128)) for r in range(count)]
    wide = jnp.concatenate(pieces, axis=0)
    return jnp.where(iota(wide.shape, 0) % 8 == iota(wide.shape, 1) // 16, wide, 0.0)


def unpack(packed, offset):
    pick = iota((128, 128), 0) % 16 == iota((128, 128), 1) - offset
    return exact_dot(spread_rows(packed), pick.astype(F32))


def kron_rows(values):
    count = values.shape[0]
    pieces = [jnp.broadcast_to(values[n : n + 1], (8, 128)) for n in range(count)]
    wide = jnp.concatenate(pieces, axis=0)
    return jnp.where(iota(wide.shape, 0) % 8 == iota(wide.shape, 1) % 8, wide, 0.0)


def put_copies(out_ref, value):
    for n in range(out_ref.shape[0]):
        out_ref[n] = value


def add_up(ref):
    total = ref[0]
    for n in range(1, ref.shape[0]):
        total = total + ref[n]
    return total


def faces_kernel(cond, pinned, x_lo, x_hi, y_lo, y_hi, scaling, keep, coef, edge):
    g = lax.axis_index("grp_0") * 4 + lax.axis_index("grp_1")
    s = (lax.axis_index("sub_0") * 4 + lax.axis_index("sub_1")) * 2 + lax.axis_index("sub_2")

    def inside(count, flag):
        return jnp.broadcast_to(flag.astype(F32), (count, CZ))

    has_x_lo, has_x_hi = inside(CY, g > 0), inside(CY, g < N_GRP - 1)
    has_y_lo, has_y_hi = inside(1, s > 0), inside(1, s < N_SUB - 1)
    rows = iota((CY, CZ), 0)
    lanes = iota((CY, CZ), 1)

    def down(v, edge):
        return jnp.where(rows == 0, edge, pltpu.roll(v, 1, 0))

    def up(v, edge):
        return jnp.where(rows == CY - 1, edge, pltpu.roll(v, CY - 1, 0))

    def left(v):
        return jnp.where(lanes == 0, 0.0, pltpu.roll(v, 1, 1))

    def right(v):
        return jnp.where(lanes == CZ - 1, 0.0, pltpu.roll(v, CZ - 1, 1))

    for x in range(CX):
        keep[x] = 1.0 - pinned[x].astype(F32)
    for x in range(CX):
        c, k = cond[x], keep[x]
        c_lo = cond[x - 1] if x else has_x_lo * x_lo[...]
        c_hi = cond[x + 1] if x < CX - 1 else has_x_hi * x_hi[...]
        k_lo = keep[x - 1] if x else has_x_lo
        k_hi = keep[x + 1] if x < CX - 1 else has_x_hi
        beside = [
            (c_lo, k_lo),
            (c_hi, k_hi),
            (down(c, has_y_lo * y_lo[x : x + 1]), down(k, has_y_lo)),
            (up(c, has_y_hi * y_hi[x : x + 1]), up(k, has_y_hi)),
            (left(c), left(k)),
            (right(c), right(k)),
        ]
        centre = None
        for n, (other, mask) in enumerate(beside):
            face = 0.5 * (c + other)
            centre = face if centre is None else centre + face
            coef[n, x] = (k * mask) * face
        edge[0, x : x + 1] = coef[2, x, 0:1]
        edge[1, x : x + 1] = coef[3, x, CY - 1 : CY]
        coef[2, x, 0:1] = jnp.zeros((1, CZ), F32)
        coef[3, x, CY - 1 : CY] = jnp.zeros((1, CZ), F32)
        whole = k * centre + (1.0 - k)
        coef[6, x] = whole
        scaling[x] = 1.0 / whole


CHUNKS = 4
DEEP = CX // CHUNKS


def chunk_copies(pairs, sems):
    return [
        [
            pltpu.make_async_copy(
                src.at[:, pl.ds(c * DEEP, DEEP)], dst.at[:, pl.ds(c * DEEP, DEEP)], sems.at[c, n]
            )
            for n, (src, dst) in enumerate(pairs)
        ]
        for c in range(CHUNKS)
    ]


def start_all(copies):
    for chunk in copies:
        for copy in chunk:
            copy.start()


def wait_all(chunk):
    for copy in chunk:
        copy.wait()


def restrict_kernel(basis_hbm, field_hbm, out, basis, field, total, sems):
    copies = chunk_copies(((basis_hbm, basis), (field_hbm, field)), sems)
    start_all(copies)
    total[...] = jnp.zeros_like(total)
    for c in range(CHUNKS):
        wait_all(copies[c])
        for x in range(c * DEEP, (c + 1) * DEEP):
            total[...] += dot3(split(slab(basis, x)), split(slab(field, x)), True)
    packed = jnp.concatenate([pack(total[...]), jnp.zeros((4, 128), F32)], axis=0)
    put_copies(out, packed)


def coarse_kernel(gathered, inverse, out, wide):
    for s in range(N_SUB):
        wide[32 * s : 32 * s + 32] = spread_rows(gathered[s, 0:4])
    rows = inverse[...].reshape(N_GRP * VEC, N_SUB * VEC)
    partial = dot3(split(rows), split(wide[...]), False)
    merge = (iota((128, 128), 0) % 16 == iota((128, 128), 1) % 16).astype(F32)
    partial = exact_dot(partial, merge)
    mine = iota(partial.shape, 0) % 8 == iota(partial.shape, 1) // 16
    partial = jnp.where(mine, partial, 0.0).reshape(N_GRP * 4, 8, 128).sum(axis=1)
    carried = add_up(gathered)[4:8]
    for g in range(N_GRP):
        out[g] = jnp.concatenate([partial[4 * g : 4 * g + 4], carried], axis=0)


def prolong_kernel(
    arrived, basis_hbm, field_hbm, scaling, keep, out, x_lo, x_hi, y_lo, y_hi, carried,
    basis, field, sems,
):
    copies = chunk_copies(((basis_hbm, basis), (field_hbm, field)), sems)
    start_all(copies)
    total = add_up(arrived)
    carried[...] = total
    pick = iota((128, 128), 0) % 16 == iota((128, 128), 1) // 8
    values = exact_dot(spread_rows(total[0:4]), pick.astype(F32))
    matrix = split(kron_rows(values).T)
    for c in range(CHUNKS):
        wait_all(copies[c])
        for x in range(c * DEEP, (c + 1) * DEEP):
            product = dot3(matrix, split(slab(basis, x)), False)
            halves = []
            for h in range(2):
                cells = slice(8 * h, 8 * h + 8)
                coarse = product[:, CZ * h : CZ * h + CZ].reshape(SRC, 8, CZ)
                halves.append(scaling[x, cells, :] * field[:, x, cells, :] + coarse)
                out[:, x, cells, :] = halves[h]
            y_lo[:, x : x + 1, :] = keep[x, 0:1, :] * halves[0][:, 0:1, :]
            y_hi[:, x : x + 1, :] = keep[x, 15:16, :] * halves[1][:, 7:8, :]
            for edge, face in ((0, x_lo), (CX - 1, x_hi)):
                if x == edge:
                    face[:, 0:8, :] = keep[x, 0:8, :] * halves[0]
                    face[:, 8:16, :] = keep[x, 8:16, :] * halves[1]


def inner_kernel(field, coef, image):
    def plane(x, low, high):
        for j in range(SRC):
            v = field[j, x]
            beside = coef[2, x] * pltpu.roll(v, 1, 0) + coef[3, x] * pltpu.roll(v, CY - 1, 0)
            beside = beside + coef[4, x] * pltpu.roll(v, 1, 1)
            beside = beside + coef[5, x] * pltpu.roll(v, CZ - 1, 1)
            if low:
                beside = beside + coef[0, x] * field[j, x - 1]
            if high:
                beside = beside + coef[1, x] * field[j, x + 1]
            image[j, x] = coef[6, x] * v - beside

    def middle(i, carry):
        plane(2 * i + 1, True, True)
        plane(2 * i + 2, True, True)
        return carry

    plane(0, False, True)
    lax.fori_loop(0, CX // 2 - 1, middle, 0)
    plane(CX - 1, True, False)


def whole_plane(x, inner, y_lo, y_hi, edge):
    rows = iota((8, CZ), 0)
    low = jnp.where(rows == 0, edge[0, pl.ds(x, 1), :] * y_lo[:, pl.ds(x, 1), :], 0.0)
    high = jnp.where(rows == 7, edge[1, pl.ds(x, 1), :] * y_hi[:, pl.ds(x, 1), :], 0.0)
    return inner[:, x, 0:8, :] - low, inner[:, x, 8:16, :] - high


def side_by_side(halves):
    return jnp.concatenate([h.reshape(SRC * 8, CZ) for h in halves], axis=1)


def by_chunks(plane, inner, image, arriving, copies):
    for c in range(CHUNKS):
        wait_all(arriving[c])
        for x in range(c * DEEP, (c + 1) * DEEP):
            plane(x, image if x in (0, CX - 1) else inner)
        for copy in copies[c]:
            copy.start()
    for c in range(CHUNKS):
        wait_all(copies[c])


def first_image_kernel(
    inner, x_lo, x_hi, y_lo, y_hi, coef, edge, field, basis_hbm, right_side_hbm, image_hbm, out,
    image, total, gram, basis, right_side, sems, in_sems,
):
    arriving = chunk_copies(((basis_hbm, basis), (right_side_hbm, right_side)), in_sems)
    start_all(arriving)
    image[:, 0] = inner[:, 0] - coef[0, 0] * x_lo[...]
    image[:, CX - 1] = inner[:, CX - 1] - coef[1, CX - 1] * x_hi[...]
    total[...] = jnp.zeros_like(total)
    gram[...] = jnp.zeros_like(gram)

    def plane(x, source):
        halves = whole_plane(x, source, y_lo, y_hi, edge)
        image[:, x, 0:8, :], image[:, x, 8:16, :] = halves
        applied = split(side_by_side(halves))
        direction = split(slab(field, x))
        total[...] += dot3(rows_of(split(slab(basis, x)), direction), applied, True)
        gram[...] += dot3(direction, split(slab(right_side, x)), True)

    by_chunks(plane, inner, image, arriving, chunk_copies(((image, image_hbm),), sems))
    packed = [pack(total[0 : VEC * 8]), pack(gram[...]), pack(total[VEC * 8 :])]
    put_copies(out, jnp.concatenate(packed, axis=0))


def second_image_kernel(
    inner, x_lo, x_hi, y_lo, y_hi, coef, edge, field, first_image_hbm, image_hbm, out,
    image, total, first_image, sems, in_sems,
):
    arriving = chunk_copies(((first_image_hbm, first_image),), in_sems)
    start_all(arriving)
    image[:, 0] = inner[:, 0] - coef[0, 0] * x_lo[...]
    image[:, CX - 1] = inner[:, CX - 1] - coef[1, CX - 1] * x_hi[...]
    total[...] = jnp.zeros_like(total)

    def plane(x, source):
        halves = whole_plane(x, source, y_lo, y_hi, edge)
        image[:, x, 0:8, :], image[:, x, 8:16, :] = halves
        pair = rows_of(split(slab(first_image, x)), split(side_by_side(halves)))
        total[...] += dot3(pair, split(slab(field, x)), True)

    by_chunks(plane, inner, image, arriving, chunk_copies(((image, image_hbm),), sems))
    cross = total[0:128]
    packed = [pack(cross), pack(cross.T), pack(total[128:256]), jnp.zeros((2, 128), F32)]
    put_copies(out, jnp.concatenate(packed, axis=0))


def relay_kernel(arrived, out):
    put_copies(out, add_up(arrived))


def eliminate(matrix):
    rows = iota(matrix.shape, 0)
    for p in range(16):
        row = matrix[p : p + 1] / matrix[p : p + 1, p : p + 1]
        column = matrix[:, p : p + 1]
        matrix = jnp.where(rows == p, row, matrix - column * row)
    return matrix


def tall(matrix):
    return jnp.concatenate([matrix, jnp.zeros((112, 128), F32)], axis=0)


def early_kernel(carried, out):
    projection, curvature = carried[4:6], carried[6:8]
    unit = (iota((16, 128), 0) == iota((16, 128), 1) - 32).astype(F32)
    out[...] = eliminate(unpack(curvature, 0) + unpack(projection, 16) + unit)


def finish_kernel(
    arrived, carried, early, first_hbm, second_hbm, first_image_hbm, second_image_hbm,
    right_side_hbm, solution_hbm, residual_hbm,
    first, second, first_image, second_image, right_side, solution, residual, sems, out_sems,
):
    copies = chunk_copies(
        (
            (first_hbm, first),
            (second_hbm, second),
            (first_image_hbm, first_image),
            (second_image_hbm, second_image),
            (right_side_hbm, right_side),
        ),
        sems,
    )
    start_all(copies)
    total = add_up(arrived)
    cross, crossed, energy = total[0:2], total[2:4], total[4:6]
    curvature = carried[6:8]
    lanes = iota((16, 128), 1)
    early_part = early[...]
    inverse = jnp.where(lanes < 16, pltpu.roll(early_part, 96, 1), 0.0)
    mixed = exact_dot(inverse, tall(unpack(cross, 32)))
    solved = jnp.where(lanes < 32, early_part, mixed)
    back = exact_dot(unpack(crossed, 0), tall(solved))
    reduced = unpack(energy, 0) - pltpu.roll(back, 96, 1)
    target = back - unpack(curvature, 16)
    last = eliminate(jnp.where(lanes < 16, reduced, jnp.where(lanes < 32, target, 0.0)))
    mix = jnp.where(lanes < 16, pltpu.roll(mixed, 96, 1), 0.0)
    on_first = early_part + exact_dot(mix, tall(last))
    pick = (iota((128, 128), 0) - 16 == iota((128, 128), 1) // 8).astype(F32)
    on_first = kron_rows(exact_dot(on_first, pick))
    on_second = kron_rows(exact_dot(-last, pick))
    matrix = split(jnp.concatenate([on_first, on_second], axis=0).T)

    out_copies = chunk_copies(((solution, solution_hbm), (residual, residual_hbm)), out_sems)
    for c in range(CHUNKS):
        wait_all(copies[c])
        for x in range(c * DEEP, (c + 1) * DEEP):
            pair = rows_of(split(slab(first, x)), split(slab(second, x)))
            images = rows_of(split(slab(first_image, x)), split(slab(second_image, x)))
            moved, removed = dot3(matrix, pair, False), dot3(matrix, images, False)
            for h in range(2):
                cells = slice(8 * h, 8 * h + 8)
                part = slice(CZ * h, CZ * h + CZ)
                solution[:, x, cells, :] = moved[:, part].reshape(SRC, 8, CZ)
                left_over = right_side[:, x, cells, :] - removed[:, part].reshape(SRC, 8, CZ)
                residual[:, x, cells, :] = left_over
        for copy in out_copies[c]:
            copy.start()
    for c in range(CHUNKS):
        wait_all(out_copies[c])


VMEM, HBM = pltpu.VMEM, pltpu.HBM
MIB = 1024 * 1024
FULL_LIMIT, PROLONG_LIMIT, IMAGE_LIMIT = 58, 50, 46


def call(kernel, outs, scratch, *args, far=(), limit=16):
    specs = [
        pl.BlockSpec(memory_space=HBM if n in far else VMEM) for n in range(len(args) + len(outs))
    ]
    return pl.pallas_call(
        kernel,
        out_shape=[jax.ShapeDtypeStruct(shape, F32) for shape in outs],
        in_specs=specs[: len(args)],
        out_specs=specs[len(args) :],
        scratch_shapes=[pltpu.VMEM(s, F32) if isinstance(s, tuple) else s for s in scratch],
        compiler_params=pltpu.CompilerParams(vmem_limit_bytes=limit * MIB),
    )(*args)


def exchange(pieces, axes):
    return lax.all_to_all(pieces, axes, split_axis=0, concat_axis=0, tiled=True)


def swap_edges(low, high, axes):
    count = lax.axis_size(axes)
    up = [(i, (i + 1) % count) for i in range(count)]
    return lax.ppermute(high, axes, up), lax.ppermute(low, axes, [(b, a) for a, b in up])


def copy_sems(count):
    return pltpu.SemaphoreType.DMA((CHUNKS, count))


def local(right_side, conductivity, pinned_cells, coarse_basis, coarse_inverse):
    face = (SRC, CY, CZ)
    block = (CX, CY, CZ)
    tile = (8, 128)
    bases = (VEC, *block)

    def coarse_answer(pieces):
        gathered = exchange(pieces, SUB)
        (partial,) = call(
            coarse_kernel, [(N_GRP, *tile)], [(N_SUB * VEC, 128)], gathered, coarse_inverse
        )
        return exchange(partial, GRP)

    def precondition(pieces, field):
        smoothed, x_lo, x_hi, y_lo, y_hi, carried = call(
            prolong_kernel,
            [FIELD, face, face, face, face, tile],
            [bases, FIELD, copy_sems(2)],
            coarse_answer(pieces),
            coarse_basis,
            field,
            scaling,
            keep,
            far=(1, 2),
            limit=PROLONG_LIMIT,
        )
        edges = (*swap_edges(x_lo, x_hi, GRP), *swap_edges(y_lo, y_hi, SUB))
        (inner,) = call(inner_kernel, [FIELD], [], smoothed, coef)
        return smoothed, (inner, *edges, coef, edge), carried

    x_edges = swap_edges(conductivity[0], conductivity[-1], GRP)
    y_edges = swap_edges(conductivity[:, 0], conductivity[:, -1], SUB)
    (pieces,) = call(
        restrict_kernel,
        [(N_SUB, *tile)],
        [bases, FIELD, (VEC * 8, 128), copy_sems(2)],
        coarse_basis,
        right_side,
        far=(0, 1),
        limit=FULL_LIMIT,
    )
    scaling, keep, coef, edge = call(
        faces_kernel,
        [block, block, (7, *block), (2, CX, CZ)],
        [],
        conductivity,
        pinned_cells,
        *x_edges,
        *y_edges,
    )
    first, inner, _ = precondition(pieces, right_side)
    first_image, pieces = call(
        first_image_kernel,
        [FIELD, (N_SUB, *tile)],
        [FIELD, (VEC * 8 + 128, 128), (128, 128), bases, FIELD, copy_sems(1), copy_sems(2)],
        *inner,
        first,
        coarse_basis,
        right_side,
        far=(8, 9, 10),
        limit=IMAGE_LIMIT,
    )
    second, inner, carried = precondition(pieces, first_image)
    (early,) = call(early_kernel, [(16, 128)], [], carried)
    second_image, pieces = call(
        second_image_kernel,
        [FIELD, (N_GRP, *tile)],
        [FIELD, (256, 128), FIELD, copy_sems(1), copy_sems(1)],
        *inner,
        second,
        first_image,
        far=(8, 9),
        limit=IMAGE_LIMIT,
    )
    (pieces,) = call(relay_kernel, [(N_SUB, *tile)], [], exchange(pieces, GRP))
    return tuple(
        call(
            finish_kernel,
            [FIELD, FIELD],
            [FIELD] * 7 + [copy_sems(5), copy_sems(2)],
            exchange(pieces, SUB),
            carried,
            early,
            first,
            second,
            first_image,
            second_image,
            right_side,
            far=(3, 4, 5, 6, 7, 8, 9),
            limit=FULL_LIMIT,
        )
    )


def solution(mesh):
    split_mesh = Mesh(
        mesh.devices.reshape(2, 4, 4, 4, 2), ("grp_0", "grp_1", "sub_0", "sub_1", "sub_2")
    )
    in_specs = (
        P(None, GRP, SUB, None),
        P(GRP, SUB, None),
        P(GRP, SUB, None),
        P(None, GRP, SUB, None),
        P(None, SUB, GRP),
    )
    out_specs = (P(None, GRP, SUB, None), P(None, GRP, SUB, None))
    return jax.shard_map(
        local, mesh=split_mesh, in_specs=in_specs, out_specs=out_specs, check_vma=False
    )
```

time: 181 us -> 160 us (0.88)
  blocking collectives: 61 us -> 38.3 us
  Pallas kernels: 57.2 us -> 41.8 us
  starting transfers between devices: 34.3 us -> 46.6 us
  waiting for transfers between devices: 22.3 us -> 27.4 us
    all_to_all x4 -> x3, blocking collectives: 61 us -> 38.3 us  [exchange(): return lax.all_to_all(pieces, axes, split_axis=0, concat_axis=0, tiled=True)]
    pallas_call x10 -> x13, Pallas kernels: 57.2 us -> 41.8 us  [call(): pl.pallas_call(kernel, out_shape=[jax.ShapeDtypeStruct(shape, F32) for sh...]
    all_to_all x2 -> x3, starting transfers between devices: 17.1 us -> 29.3 us  [exchange(): return lax.all_to_all(pieces, axes, split_axis=0, concat_axis=0, tiled=True)]
    all_to_all x2 -> x3, waiting for transfers between devices: 9.23 us -> 17.8 us  [exchange(): return lax.all_to_all(pieces, axes, split_axis=0, concat_axis=0, tiled=True)]
    ppermute x6, waiting for transfers between devices: 7.39 us -> 3.91 us  [swap_edges(): lax.ppermute(high, axes, up)]
    unnamed x18 -> x22, local copies, waits for them, and re-layouts: 4.73 us -> 4.05 us
  transfers between devices with their start and end apart: 14 -> 15, of which waited for: 8 -> 7; matrix products, arithmetic and copies ran while one was open for 0% -> 0% of each run, Pallas kernels for 1% -> 4%
where the time goes in v1:
time: 160 us; the launch traced here: 159 us
  starting transfers between devices  46.6 us (29%)
  Pallas kernels  41.8 us (26%)
  blocking collectives  38.3 us (24%)
  waiting for transfers between devices  27.4 us (17%)
  local copies, waits for them, and re-layouts  4.07 us (3%)
    pallas_call x13, Pallas kernels, call(): pl.pallas_call(kernel, out_shape=[jax.ShapeDtypeStruct(shape, F32) for sh...  41.8 us
    all_to_all x3, blocking collectives, exchange(): return lax.all_to_all(pieces, axes, split_axis=0, concat_axis=0, tiled=True)  38.3 us
    all_to_all x3, starting transfers between devices, exchange(): return lax.all_to_all(pieces, axes, split_axis=0, concat_axis=0, tiled=True)  29.3 us
    all_to_all x3, waiting for transfers between devices, exchange(): return lax.all_to_all(pieces, axes, split_axis=0, concat_axis=0, tiled=True)  17.8 us
    ppermute x6, starting transfers between devices, swap_edges(): lax.ppermute(low, axes, [(b, a) for a, b in up])  10.7 us
    ppermute x6, starting transfers between devices, swap_edges(): lax.ppermute(high, axes, up)  6.62 us
    ppermute x6, waiting for transfers between devices, swap_edges(): lax.ppermute(low, axes, [(b, a) for a, b in up])  5.66 us
    unnamed x22, local copies, waits for them, and re-layouts  4.05 us
  transfers between devices with their start and end apart: 15, of which 7 were waited for; matrix products, arithmetic and copies ran while one was open for 0% of the time, Pallas kernels for 4%

profile of v1, /device:TPU:1, one launch (start us, length us, event | category | flops | bytes accessed | tf_op | source)
XLA Modules:
  0.0 159.2 jit_solution(12195042194443869563)
XLA Ops:
  0.6 0.0 copy-start.6
  0.6 0.0 copy-start.3
  0.7 0.0 copy-start.7
  0.7 6.0 %shard_map.68 = f32[32,8,128]{2,1,0:T(8,128)} custom-call(f32[32,16,16,128]{3,2,1,0:T(8,128)} %basis_hbm.7, f32[16,16,16,128]{3,2,1,0:T(8,128)} %right_side_hbm.3), custom_call_target="tpu_custom_call" | custom-call | tf_op jit(solution)/shard_map/pallas_call | solution.py:402
  6.6 12.6 %all-to-all-start = ((f32[32,8,128]{2,1,0:T(8,128)}), f32[32,8,128]{2,1,0:T(8,128)S(1)}, u32[]{:S(2)}, u32[]{:S(2)}) async-start(f32[32,8,128]{2,1,0:T(8,128)} %shard_map.68), calls=%async_computation | async-start | bytes 262144 | tf_op jit(solution)/shard_map/all_to_all | solution.py:413
  19.2 0.0 copy-done.6
  19.3 1.7 %collective-permute-start.2 = (f32[16,128]{1,0:T(8,128)S(1)}, f32[16,128]{1,0:T(8,128)S(1)}, u32[]{:S(2)}, u32[]{:S(2)}) collective-permute-start(f32[16,128]{1,0:T(8,128)S(1)} %bitcast.11), channel_id=1, source_target_pairs={{0,1},{1,2},{2,3},{3,4},{4,5},{5,6},{6,7},{7,8},{8,9},{9,10},{10,1... | collective-permute-start | bytes 24584 | tf_op jit(solution)/shard_map/ppermute | solution.py:419
  21.0 0.0 collective-permute-start.3
  21.0 9.2 %all-to-all-done.gathered = f32[32,8,128]{2,1,0:T(8,128)S(1)} async-done(((f32[32,8,128]{2,1,0:T(8,128)}), f32[32,8,128]{2,1,0:T(8,128)S(1)}, u32[]{:S(2)}, u32[]{:S(2)}) %all-to-all-start) | async-done | bytes 131104 | tf_op jit(solution)/shard_map/all_to_all | solution.py:413
  30.2 0.0 copy-done.3
  30.2 1.6 shard_map.69
  31.8 4.5 %all-to-all-start.1 = ((f32[8,8,128]{2,1,0:T(8,128)}), f32[8,8,128]{2,1,0:T(8,128)S(1)}, u32[]{:S(2)}, u32[]{:S(2)}) async-start(f32[8,8,128]{2,1,0:T(8,128)} %shard_map.69), calls=%async_computation.1 | async-start | bytes 65536 | tf_op jit(solution)/shard_map/all_to_all | solution.py:413
  36.3 3.6 %collective-permute-start.1 = (f32[16,128]{1,0:T(8,128)S(1)}, f32[16,128]{1,0:T(8,128)S(1)}, u32[]{:S(2)}, u32[]{:S(2)}) collective-permute-start(f32[16,128]{1,0:T(8,128)S(1)} %get-tuple-element.42), channel_id=1, source_target_pairs={{32,0},{64,32},{96,64},{128,96},{160,128},{192,160},{224,192},{0,2... | collective-permute-start | bytes 24584 | tf_op jit(solution)/shard_map/ppermute | solution.py:419
  39.9 0.0 collective-permute-start
  39.9 0.0 collective-permute-done.2.y_lo
  39.9 0.0 collective-permute-done.3.y_hi
  39.9 0.8 collective-permute-done.1.x_hi
  40.7 3.8 %collective-permute-done.x_lo = f32[16,128]{1,0:T(8,128)S(1)} collective-permute-done((f32[16,128]{1,0:T(8,128)S(1)}, f32[16,128]{1,0:T(8,128)S(1)}, u32[]{:S(2)}, u32[]{:S(2)}) %collective-permute-start) | collective-permute-done | bytes 8224 | tf_op jit(solution)/shard_map/ppermute | solution.py:419
  44.5 0.0 copy-done.7
  44.5 0.3 shard_map.70
  44.8 0.0 all-to-all-done.1.arrived
  44.8 3.5 %shard_map.71 = (f32[16,16,16,128]{3,2,1,0:T(8,128)S(1)}, f32[16,16,128]{2,1,0:T(8,128)S(1)}, f32[16,16,128]{2,1,0:T(8,128)S(1)}, f32[16,16,128]{2,1,0:T(8,128)S...) custom-call(f32[8,8,128]{2,1,0:T(8,128)S(1)} %all-to-all-done.1.arrived, f32[32,16,16,128]{3,2,1,0:T(8,128)} %basis_hbm.7, ...), custom_call_target="tpu_custom_call" | custom-call | tf_op jit(solution)/shard_map/pallas_call | solution.py:402
  48.3 0.0 copy-start.1
  48.3 0.1 collective-permute-start.4
  48.4 3.6 %collective-permute-start.5 = (f32[16,16,128]{2,1,0:T(8,128)S(1)}, f32[16,16,128]{2,1,0:T(8,128)S(1)}, u32[]{:S(2)}, u32[]{:S(2)}) collective-permute-start(f32[16,16,128]{2,1,0:T(8,128)S(1)} %get-tuple-element.26), channel_id=1, source_target_pairs={{32,0},{64,32},{96,64},{128,96},{160,128},{192,160},{224,192},{0,2... | collective-permute-start | bytes 393224 | tf_op jit(solution)/shard_map/ppermute | solution.py:419
  51.9 2.7 %collective-permute-start.6 = (f32[16,16,128]{2,1,0:T(8,128)S(1)}, f32[16,16,128]{2,1,0:T(8,128)S(1)}, u32[]{:S(2)}, u32[]{:S(2)}) collective-permute-start(f32[16,16,128]{2,1,0:T(8,128)S(1)} %get-tuple-element.27), channel_id=1, source_target_pairs={{0,1},{1,2},{2,3},{3,4},{4,5},{5,6},{6,7},{7,8},{8,9},{9,10},{10,1... | collective-permute-start | bytes 393224 | tf_op jit(solution)/shard_map/ppermute | solution.py:419
  54.7 0.1 collective-permute-start.7
  54.8 1.7 %shard_map.72.inner = f32[16,16,16,128]{3,2,1,0:T(8,128)S(1)} custom-call(f32[16,16,16,128]{3,2,1,0:T(8,128)S(1)} %get-tuple-element.23.field.first_hbm, f32[7,16,16,128]{3,2,1,0:T(8,128)S(1)} %get-tuple-element.24.coef), custom_call_target="tpu_custom_call" | custom-call | tf_op jit(solution)/shard_map/pallas_call | solution.py:402
  56.5 0.0 collective-permute-done.4.x_lo
  56.5 0.0 collective-permute-done.5.x_hi
  56.5 0.1 collective-permute-done.6.y_lo
  56.6 2.4 %collective-permute-done.7.y_hi = f32[16,16,128]{2,1,0:T(8,128)S(1)} collective-permute-done((f32[16,16,128]{2,1,0:T(8,128)S(1)}, f32[16,16,128]{2,1,0:T(8,128)S(1)}, u32[]{:S(2)}, u32[]{:S(2)}) %collective-permute-start.7) | collective-permute-done | bytes 131104 | tf_op jit(solution)/shard_map/ppermute | solution.py:419
  59.1 0.0 copy-done.1
  59.1 7.5 %shard_map.73 = (f32[16,16,16,128]{3,2,1,0:T(8,128)S(1)}, f32[32,8,128]{2,1,0:T(8,128)S(1)}) custom-call(f32[16,16,16,128]{3,2,1,0:T(8,128)S(1)} %shard_map.72.inner, f32[16,16,128]{2,1,0:T(8,128)S(1)} %collective-permute-done.4.x_lo, f32[16,16,128]{2,1,0:T(8,128)S(1)} %collective-permute-done.5.x_hi, f32[16,16,128]{2,1,0:T(8,128)S(1)} %collective-permute-done.6.y_lo, ...), custom_call_target="tpu_custom_call" | custom-call | tf_op jit(solution)/shard_map/pallas_call | solution.py:402
  66.6 0.0 copy-start
  66.6 1.3 copy-done
  67.9 23.3 %all_to_all.30.gathered = f32[32,8,128]{2,1,0:T(8,128)S(1)} all-to-all(f32[32,8,128]{2,1,0:T(8,128)S(1)} %get-tuple-element.30), channel_id=1, replica_groups=mesh['grp_0'=2,'grp_1'=4,'sub_0'=4,'sub_1'=4,'sub_2'=2] {'sub_0','sub_1'..., dimensions={0} | all-to-all | bytes 262144 | tf_op jit(solution)/shard_map/all_to_all | solution.py:413
  91.2 0.0 copy-done.4
  91.2 1.0 shard_map.74
  92.2 7.5 %all_to_all.31.arrived = f32[8,8,128]{2,1,0:T(8,128)S(1)} all-to-all(f32[8,8,128]{2,1,0:T(8,128)S(1)} %shard_map.74), channel_id=1, replica_groups=mesh['grp_0'=2,'grp_1'=4,'sub_0'=4,'sub_1'=4,'sub_2'=2] {'grp_0','grp_1'}, dimensions={0} | all-to-all | bytes 65536 | tf_op jit(solution)/shard_map/all_to_all | solution.py:413
  99.7 3.3 %shard_map.75 = (f32[16,16,16,128]{3,2,1,0:T(8,128)S(1)}, f32[16,16,128]{2,1,0:T(8,128)S(1)}, f32[16,16,128]{2,1,0:T(8,128)S(1)}, f32[16,16,128]{2,1,0:T(8,128)S...) custom-call(f32[8,8,128]{2,1,0:T(8,128)S(1)} %all_to_all.31.arrived, f32[32,16,16,128]{3,2,1,0:T(8,128)} %basis_hbm.7, ...), custom_call_target="tpu_custom_call" | custom-call | tf_op jit(solution)/shard_map/pallas_call | solution.py:402
  103.0 0.0 copy-start.2
  103.0 0.0 copy-start.9
  103.0 0.4 collective-permute-start.8
  103.4 3.3 %collective-permute-start.9 = (f32[16,16,128]{2,1,0:T(8,128)S(1)}, f32[16,16,128]{2,1,0:T(8,128)S(1)}, u32[]{:S(2)}, u32[]{:S(2)}) collective-permute-start(f32[16,16,128]{2,1,0:T(8,128)S(1)} %get-tuple-element.34), channel_id=1, source_target_pairs={{32,0},{64,32},{96,64},{128,96},{160,128},{192,160},{224,192},{0,2... | collective-permute-start | bytes 393224 | tf_op jit(solution)/shard_map/ppermute | solution.py:419
  106.7 1.7 %collective-permute-start.10 = (f32[16,16,128]{2,1,0:T(8,128)S(1)}, f32[16,16,128]{2,1,0:T(8,128)S(1)}, u32[]{:S(2)}, u32[]{:S(2)}) collective-permute-start(f32[16,16,128]{2,1,0:T(8,128)S(1)} %get-tuple-element.35), channel_id=1, source_target_pairs={{0,1},{1,2},{2,3},{3,4},{4,5},{5,6},{6,7},{7,8},{8,9},{9,10},{10,1... | collective-permute-start | bytes 393224 | tf_op jit(solution)/shard_map/ppermute | solution.py:419
  108.3 0.2 collective-permute-start.11
  108.6 1.7 %shard_map.76.inner = f32[16,16,16,128]{3,2,1,0:T(8,128)S(1)} custom-call(f32[16,16,16,128]{3,2,1,0:T(8,128)S(1)} %get-tuple-element.32.field.second_hbm, f32[7,16,16,128]{3,2,1,0:T(8,128)S(1)} %get-tuple-element.24.coef), custom_call_target="tpu_custom_call" | custom-call | tf_op jit(solution)/shard_map/pallas_call | solution.py:402
  110.3 0.0 collective-permute-done.8.x_lo
  110.3 0.0 collective-permute-done.9.x_hi
  110.3 0.0 collective-permute-done.10.y_lo
  110.3 2.4 %collective-permute-done.11.y_hi = f32[16,16,128]{2,1,0:T(8,128)S(1)} collective-permute-done((f32[16,16,128]{2,1,0:T(8,128)S(1)}, f32[16,16,128]{2,1,0:T(8,128)S(1)}, u32[]{:S(2)}, u32[]{:S(2)}) %collective-permute-start.11) | collective-permute-done | bytes 131104 | tf_op jit(solution)/shard_map/ppermute | solution.py:419
  112.7 0.0 copy-done.2
  112.7 5.1 %shard_map.77 = (f32[16,16,16,128]{3,2,1,0:T(8,128)S(1)}, f32[8,8,128]{2,1,0:T(8,128)S(1)}) custom-call(f32[16,16,16,128]{3,2,1,0:T(8,128)S(1)} %shard_map.76.inner, f32[16,16,128]{2,1,0:T(8,128)S(1)} %collective-permute-done.8.x_lo, f32[16,16,128]{2,1,0:T(8,128)S(1)} %collective-permute-done.9.x_hi, f32[16,16,128]{2,1,0:T(8,128)S(1)} %collective-permute-done.10.y_lo, ...), custom_call_target="tpu_custom_call" | custom-call | tf_op jit(solution)/shard_map/pallas_call | solution.py:402
  117.8 0.0 copy-start.5
  117.8 1.4 copy-done.5
  119.2 7.5 %all_to_all.32.arrived = f32[8,8,128]{2,1,0:T(8,128)S(1)} all-to-all(f32[8,8,128]{2,1,0:T(8,128)S(1)} %get-tuple-element.37), channel_id=1, replica_groups=mesh['grp_0'=2,'grp_1'=4,'sub_0'=4,'sub_1'=4,'sub_2'=2] {'grp_0','grp_1'}, dimensions={0} | all-to-all | bytes 65536 | tf_op jit(solution)/shard_map/all_to_all | solution.py:413
  126.7 0.7 shard_map.78
  127.4 12.2 %all-to-all-start.5 = ((f32[32,8,128]{2,1,0:T(8,128)}), f32[32,8,128]{2,1,0:T(8,128)S(1)}, u32[]{:S(2)}, u32[]{:S(2)}) async-start(f32[32,8,128]{2,1,0:T(8,128)} %shard_map.78), calls=%async_computation.5 | async-start | bytes 262144 | tf_op jit(solution)/shard_map/all_to_all | solution.py:413
  139.6 1.4 shard_map.79.early
  141.0 0.7 copy-done.8
  141.7 8.6 %all-to-all-done.5.arrived = f32[32,8,128]{2,1,0:T(8,128)S(1)} async-done(((f32[32,8,128]{2,1,0:T(8,128)}), f32[32,8,128]{2,1,0:T(8,128)S(1)}, u32[]{:S(2)}, u32[]{:S(2)}) %all-to-all-start.5) | async-done | bytes 131104 | tf_op jit(solution)/shard_map/all_to_all | solution.py:413
  150.3 0.6 copy-done.10
  150.9 8.1 %shard_map.80 = (f32[16,16,16,128]{3,2,1,0:T(8,128)}, f32[16,16,16,128]{3,2,1,0:T(8,128)}) custom-call(f32[32,8,128]{2,1,0:T(8,128)} %copy-done.10, f32[8,128]{1,0:T(8,128)} %copy-done.9, f32[16,128]{1,0:T(8,128)} %copy-done.8, f32[16,16,16,128]{3,2,1,0:T(8,128)} %copy-done.1, f32[16,16,16,128]{3,2,1,0:T(8,128)} %copy-done.2, f32[16,16,16,128]{3,2,1,0:T(8,128)} %copy-done, ...), custom_call_target="tpu_custom_call" | custom-call | tf_op jit(solution)/shard_map/pallas_call | solution.py:402
  (6 shorter events, 0.0 us)
Async XLA Ops:
  0.6 18.6 %copy-start.6 = (f32[16,16,128]{2,1,0:T(8,128)S(1)}, f32[16,16,128]{2,1,0:T(8,128)}, u32[]{:S(2)}) copy-start(f32[16,16,128]{2,1,0:T(8,128)} %cond.1) | copy-start | bytes 393220
  0.6 29.6 %copy-start.3 = (f32[8,32,1024]{2,1,0:T(8,128)S(1)}, f32[8,32,1024]{2,1,0:T(8,128)}, u32[]{:S(2)}) copy-start(f32[8,32,1024]{2,1,0:T(8,128)} %inverse.3) | copy-start | bytes 3145732
  0.7 43.8 %copy-start.7 = (s32[16,16,128]{2,1,0:T(8,128)S(1)}, s32[16,16,128]{2,1,0:T(8,128)}, u32[]{:S(2)}) copy-start(s32[16,16,128]{2,1,0:T(8,128)} %pinned.1) | copy-start | bytes 393220
  6.6 23.6 %all-to-all-start = ((f32[32,8,128]{2,1,0:T(8,128)}), f32[32,8,128]{2,1,0:T(8,128)S(1)}, u32[]{:S(2)}, u32[]{:S(2)}) async-start(f32[32,8,128]{2,1,0:T(8,128)} %shard_map.68), calls=%async_computation | async-start | bytes 262144 | tf_op jit(solution)/shard_map/all_to_all | solution.py:413
  19.3 20.6 %collective-permute-start.2 = (f32[16,128]{1,0:T(8,128)S(1)}, f32[16,128]{1,0:T(8,128)S(1)}, u32[]{:S(2)}, u32[]{:S(2)}) collective-permute-start(f32[16,128]{1,0:T(8,128)S(1)} %bitcast.11), channel_id=1, source_target_pairs={{0,1},{1,2},{2,3},{3,4},{4,5},{5,6},{6,7},{7,8},{8,9},{9,10},{10,1... | collective-permute-start | bytes 24584 | tf_op jit(solution)/shard_map/ppermute | solution.py:419
  21.0 18.9 %collective-permute-start.3 = (f32[16,128]{1,0:T(8,128)S(1)}, f32[16,128]{1,0:T(8,128)S(1)}, u32[]{:S(2)}, u32[]{:S(2)}) collective-permute-start(f32[16,128]{1,0:T(8,128)S(1)} %bitcast.10), channel_id=1, source_target_pairs={{1,0},{2,1},{3,2},{4,3},{5,4},{6,5},{7,6},{8,7},{9,8},{10,9},{11,1... | collective-permute-start | bytes 24584 | tf_op jit(solution)/shard_map/ppermute | solution.py:419
  31.8 13.0 %all-to-all-start.1 = ((f32[8,8,128]{2,1,0:T(8,128)}), f32[8,8,128]{2,1,0:T(8,128)S(1)}, u32[]{:S(2)}, u32[]{:S(2)}) async-start(f32[8,8,128]{2,1,0:T(8,128)} %shard_map.69), calls=%async_computation.1 | async-start | bytes 65536 | tf_op jit(solution)/shard_map/all_to_all | solution.py:413
  36.3 4.4 %collective-permute-start.1 = (f32[16,128]{1,0:T(8,128)S(1)}, f32[16,128]{1,0:T(8,128)S(1)}, u32[]{:S(2)}, u32[]{:S(2)}) collective-permute-start(f32[16,128]{1,0:T(8,128)S(1)} %get-tuple-element.42), channel_id=1, source_target_pairs={{32,0},{64,32},{96,64},{128,96},{160,128},{192,160},{224,192},{0,2... | collective-permute-start | bytes 24584 | tf_op jit(solution)/shard_map/ppermute | solution.py:419
  39.9 4.6 %collective-permute-start = (f32[16,128]{1,0:T(8,128)S(1)}, f32[16,128]{1,0:T(8,128)S(1)}, u32[]{:S(2)}, u32[]{:S(2)}) collective-permute-start(f32[16,128]{1,0:T(8,128)S(1)} %get-tuple-element.43), channel_id=1, source_target_pairs={{0,32},{32,64},{64,96},{96,128},{128,160},{160,192},{192,224},{224... | collective-permute-start | bytes 24584 | tf_op jit(solution)/shard_map/ppermute | solution.py:419
  48.3 10.8 %copy-start.1 = (f32[16,16,16,128]{3,2,1,0:T(8,128)}, f32[16,16,16,128]{3,2,1,0:T(8,128)S(1)}, u32[]{:S(2)}) copy-start(f32[16,16,16,128]{3,2,1,0:T(8,128)S(1)} %get-tuple-element.23.field.first_hbm) | copy-start | bytes 6291460
  48.3 8.3 %collective-permute-start.4 = (f32[16,16,128]{2,1,0:T(8,128)S(1)}, f32[16,16,128]{2,1,0:T(8,128)S(1)}, u32[]{:S(2)}, u32[]{:S(2)}) collective-permute-start(f32[16,16,128]{2,1,0:T(8,128)S(1)} %get-tuple-element.25), channel_id=1, source_target_pairs={{0,32},{32,64},{64,96},{96,128},{128,160},{160,192},{192,224},{224... | collective-permute-start | bytes 393224 | tf_op jit(solution)/shard_map/ppermute | solution.py:419
  48.4 8.2 %collective-permute-start.5 = (f32[16,16,128]{2,1,0:T(8,128)S(1)}, f32[16,16,128]{2,1,0:T(8,128)S(1)}, u32[]{:S(2)}, u32[]{:S(2)}) collective-permute-start(f32[16,16,128]{2,1,0:T(8,128)S(1)} %get-tuple-element.26), channel_id=1, source_target_pairs={{32,0},{64,32},{96,64},{128,96},{160,128},{192,160},{224,192},{0,2... | collective-permute-start | bytes 393224 | tf_op jit(solution)/shard_map/ppermute | solution.py:419
  51.9 4.7 %collective-permute-start.6 = (f32[16,16,128]{2,1,0:T(8,128)S(1)}, f32[16,16,128]{2,1,0:T(8,128)S(1)}, u32[]{:S(2)}, u32[]{:S(2)}) collective-permute-start(f32[16,16,128]{2,1,0:T(8,128)S(1)} %get-tuple-element.27), channel_id=1, source_target_pairs={{0,1},{1,2},{2,3},{3,4},{4,5},{5,6},{6,7},{7,8},{8,9},{9,10},{10,1... | collective-permute-start | bytes 393224 | tf_op jit(solution)/shard_map/ppermute | solution.py:419
  54.7 4.4 %collective-permute-start.7 = (f32[16,16,128]{2,1,0:T(8,128)S(1)}, f32[16,16,128]{2,1,0:T(8,128)S(1)}, u32[]{:S(2)}, u32[]{:S(2)}) collective-permute-start(f32[16,16,128]{2,1,0:T(8,128)S(1)} %get-tuple-element.28), channel_id=1, source_target_pairs={{1,0},{2,1},{3,2},{4,3},{5,4},{6,5},{7,6},{8,7},{9,8},{10,9},{11,1... | collective-permute-start | bytes 393224 | tf_op jit(solution)/shard_map/ppermute | solution.py:419
  59.1 32.2 %copy-start.4 = (f32[8,32,1024]{2,1,0:T(8,128)S(1)}, f32[8,32,1024]{2,1,0:T(8,128)}, u32[]{:S(2)}) copy-start(f32[8,32,1024]{2,1,0:T(8,128)} %inverse.3) | copy-start | bytes 3145732
  66.6 1.3 copy-start
  103.0 9.8 %copy-start.2 = (f32[16,16,16,128]{3,2,1,0:T(8,128)}, f32[16,16,16,128]{3,2,1,0:T(8,128)S(1)}, u32[]{:S(2)}) copy-start(f32[16,16,16,128]{3,2,1,0:T(8,128)S(1)} %get-tuple-element.32.field.second_hbm) | copy-start | bytes 6291460
  103.0 36.6 %copy-start.9 = (f32[8,128]{1,0:T(8,128)}, f32[8,128]{1,0:T(8,128)S(1)}, u32[]{:S(2)}) copy-start(f32[8,128]{1,0:T(8,128)S(1)} %get-tuple-element.38.carried) | copy-start | bytes 12292
  103.0 7.3 %collective-permute-start.8 = (f32[16,16,128]{2,1,0:T(8,128)S(1)}, f32[16,16,128]{2,1,0:T(8,128)S(1)}, u32[]{:S(2)}, u32[]{:S(2)}) collective-permute-start(f32[16,16,128]{2,1,0:T(8,128)S(1)} %get-tuple-element.33), channel_id=1, source_target_pairs={{0,32},{32,64},{64,96},{96,128},{128,160},{160,192},{192,224},{224... | collective-permute-start | bytes 393224 | tf_op jit(solution)/shard_map/ppermute | solution.py:419
  103.4 6.9 %collective-permute-start.9 = (f32[16,16,128]{2,1,0:T(8,128)S(1)}, f32[16,16,128]{2,1,0:T(8,128)S(1)}, u32[]{:S(2)}, u32[]{:S(2)}) collective-permute-start(f32[16,16,128]{2,1,0:T(8,128)S(1)} %get-tuple-element.34), channel_id=1, source_target_pairs={{32,0},{64,32},{96,64},{128,96},{160,128},{192,160},{224,192},{0,2... | collective-permute-start | bytes 393224 | tf_op jit(solution)/shard_map/ppermute | solution.py:419
  106.7 3.6 %collective-permute-start.10 = (f32[16,16,128]{2,1,0:T(8,128)S(1)}, f32[16,16,128]{2,1,0:T(8,128)S(1)}, u32[]{:S(2)}, u32[]{:S(2)}) collective-permute-start(f32[16,16,128]{2,1,0:T(8,128)S(1)} %get-tuple-element.35), channel_id=1, source_target_pairs={{0,1},{1,2},{2,3},{3,4},{4,5},{5,6},{6,7},{7,8},{8,9},{9,10},{10,1... | collective-permute-start | bytes 393224 | tf_op jit(solution)/shard_map/ppermute | solution.py:419
  108.3 4.4 %collective-permute-start.11 = (f32[16,16,128]{2,1,0:T(8,128)S(1)}, f32[16,16,128]{2,1,0:T(8,128)S(1)}, u32[]{:S(2)}, u32[]{:S(2)}) collective-permute-start(f32[16,16,128]{2,1,0:T(8,128)S(1)} %get-tuple-element.36), channel_id=1, source_target_pairs={{1,0},{2,1},{3,2},{4,3},{5,4},{6,5},{7,6},{8,7},{9,8},{10,9},{11,1... | collective-permute-start | bytes 393224 | tf_op jit(solution)/shard_map/ppermute | solution.py:419
  117.8 1.4 copy-start.5
  127.4 22.9 %all-to-all-start.5 = ((f32[32,8,128]{2,1,0:T(8,128)}), f32[32,8,128]{2,1,0:T(8,128)S(1)}, u32[]{:S(2)}, u32[]{:S(2)}) async-start(f32[32,8,128]{2,1,0:T(8,128)} %shard_map.78), calls=%async_computation.5 | async-start | bytes 262144 | tf_op jit(solution)/shard_map/all_to_all | solution.py:413
  141.0 0.7 copy-start.8
  150.3 0.6 copy-start.10

commit v2 on v1

--- a/solution.py
+++ b/solution.py
@@ -86,13 +86,24 @@
     return total
 
 
-def faces_kernel(cond, pinned, x_lo, x_hi, y_lo, y_hi, scaling, keep, coef, edge):
+def position():
     g = lax.axis_index("grp_0") * 4 + lax.axis_index("grp_1")
-    s = (lax.axis_index("sub_0") * 4 + lax.axis_index("sub_1")) * 2 + lax.axis_index("sub_2")
+    return g, (lax.axis_index("sub_0") * 4 + lax.axis_index("sub_1")) * 2 + lax.axis_index("sub_2")
+
+
+def in_order(place, first, second):
+    even = place % 2 == 0
+    return jnp.where(even, first, second), jnp.where(even, second, first)
+
+
+def faces_kernel(cond, pinned, x_a, x_b, y_a, y_b, scaling, keep, coef, edge):
+    g, s = position()
 
     def inside(count, flag):
         return jnp.broadcast_to(flag.astype(F32), (count, CZ))
 
+    x_hi, x_lo = in_order(g, x_a[...], x_b[...])
+    y_hi, y_lo = in_order(s, y_a[...], y_b[...])
     has_x_lo, has_x_hi = inside(CY, g > 0), inside(CY, g < N_GRP - 1)
     has_y_lo, has_y_hi = inside(1, s > 0), inside(1, s < N_SUB - 1)
     rows = iota((CY, CZ), 0)
@@ -114,8 +125,8 @@
         keep[x] = 1.0 - pinned[x].astype(F32)
     for x in range(CX):
         c, k = cond[x], keep[x]
-        c_lo = cond[x - 1] if x else has_x_lo * x_lo[...]
-        c_hi = cond[x + 1] if x < CX - 1 else has_x_hi * x_hi[...]
+        c_lo = cond[x - 1] if x else has_x_lo * x_lo
+        c_hi = cond[x + 1] if x < CX - 1 else has_x_hi * x_hi
         k_lo = keep[x - 1] if x else has_x_lo
         k_hi = keep[x + 1] if x < CX - 1 else has_x_hi
         beside = [
@@ -194,11 +205,12 @@
 
 
 def prolong_kernel(
-    arrived, basis_hbm, field_hbm, scaling, keep, out, x_lo, x_hi, y_lo, y_hi, carried,
+    arrived, basis_hbm, field_hbm, scaling, keep, out, x_a, x_b, y_a, y_b, carried,
     basis, field, sems,
 ):
     copies = chunk_copies(((basis_hbm, basis), (field_hbm, field)), sems)
     start_all(copies)
+    g, s = position()
     total = add_up(arrived)
     carried[...] = total
     pick = iota((128, 128), 0) % 16 == iota((128, 128), 1) // 8
@@ -214,15 +226,24 @@
                 coarse = product[:, CZ * h : CZ * h + CZ].reshape(SRC, 8, CZ)
                 halves.append(scaling[x, cells, :] * field[:, x, cells, :] + coarse)
                 out[:, x, cells, :] = halves[h]
-            y_lo[:, x : x + 1, :] = keep[x, 0:1, :] * halves[0][:, 0:1, :]
-            y_hi[:, x : x + 1, :] = keep[x, 15:16, :] * halves[1][:, 7:8, :]
-            for edge, face in ((0, x_lo), (CX - 1, x_hi)):
-                if x == edge:
-                    face[:, 0:8, :] = keep[x, 0:8, :] * halves[0]
-                    face[:, 8:16, :] = keep[x, 8:16, :] * halves[1]
+            ends = (keep[x, 0:1, :] * halves[0][:, 0:1, :], keep[x, 15:16, :] * halves[1][:, 7:8, :])
+            y_a[:, x : x + 1, :], y_b[:, x : x + 1, :] = in_order(s, ends[1], ends[0])
+    low, high = keep[0] * out[:, 0], keep[CX - 1] * out[:, CX - 1]
+    x_a[...], x_b[...] = in_order(g, high, low)
 
 
 def inner_kernel(field, coef, image):
+    inner_planes(field, coef, image)
+
+
+def inner_and_early_kernel(field, coef, carried, image, early):
+    projection, curvature = carried[4:6], carried[6:8]
+    unit = (iota((16, 128), 0) == iota((16, 128), 1) - 32).astype(F32)
+    early[...] = eliminate(unpack(curvature, 0) + unpack(projection, 16) + unit)
+    inner_planes(field, coef, image)
+
+
+def inner_planes(field, coef, image):
     def plane(x, low, high):
         for j in range(SRC):
             v = field[j, x]
@@ -245,10 +266,11 @@
     plane(CX - 1, True, False)
 
 
-def whole_plane(x, inner, y_lo, y_hi, edge):
+def whole_plane(x, s, inner, y_a, y_b, edge):
     rows = iota((8, CZ), 0)
-    low = jnp.where(rows == 0, edge[0, pl.ds(x, 1), :] * y_lo[:, pl.ds(x, 1), :], 0.0)
-    high = jnp.where(rows == 7, edge[1, pl.ds(x, 1), :] * y_hi[:, pl.ds(x, 1), :], 0.0)
+    y_hi, y_lo = in_order(s, y_a[:, x : x + 1, :], y_b[:, x : x + 1, :])
+    low = jnp.where(rows == 0, edge[0, x : x + 1, :] * y_lo, 0.0)
+    high = jnp.where(rows == 7, edge[1, x : x + 1, :] * y_hi, 0.0)
     return inner[:, x, 0:8, :] - low, inner[:, x, 8:16, :] - high
 
 
@@ -268,18 +290,20 @@
 
 
 def first_image_kernel(
-    inner, x_lo, x_hi, y_lo, y_hi, coef, edge, field, basis_hbm, right_side_hbm, image_hbm, out,
+    inner, x_a, x_b, y_a, y_b, coef, edge, field, basis_hbm, right_side_hbm, image_hbm, out,
     image, total, gram, basis, right_side, sems, in_sems,
 ):
     arriving = chunk_copies(((basis_hbm, basis), (right_side_hbm, right_side)), in_sems)
     start_all(arriving)
-    image[:, 0] = inner[:, 0] - coef[0, 0] * x_lo[...]
-    image[:, CX - 1] = inner[:, CX - 1] - coef[1, CX - 1] * x_hi[...]
+    g, s = position()
+    x_hi, x_lo = in_order(g, x_a[...], x_b[...])
+    image[:, 0] = inner[:, 0] - coef[0, 0] * x_lo
+    image[:, CX - 1] = inner[:, CX - 1] - coef[1, CX - 1] * x_hi
     total[...] = jnp.zeros_like(total)
     gram[...] = jnp.zeros_like(gram)
 
     def plane(x, source):
-        halves = whole_plane(x, source, y_lo, y_hi, edge)
+        halves = whole_plane(x, s, source, y_a, y_b, edge)
         image[:, x, 0:8, :], image[:, x, 8:16, :] = halves
         applied = split(side_by_side(halves))
         direction = split(slab(field, x))
@@ -292,17 +316,19 @@
 
 
 def second_image_kernel(
-    inner, x_lo, x_hi, y_lo, y_hi, coef, edge, field, first_image_hbm, image_hbm, out,
+    inner, x_a, x_b, y_a, y_b, coef, edge, field, first_image_hbm, image_hbm, out,
     image, total, first_image, sems, in_sems,
 ):
     arriving = chunk_copies(((first_image_hbm, first_image),), in_sems)
     start_all(arriving)
-    image[:, 0] = inner[:, 0] - coef[0, 0] * x_lo[...]
-    image[:, CX - 1] = inner[:, CX - 1] - coef[1, CX - 1] * x_hi[...]
+    g, s = position()
+    x_hi, x_lo = in_order(g, x_a[...], x_b[...])
+    image[:, 0] = inner[:, 0] - coef[0, 0] * x_lo
+    image[:, CX - 1] = inner[:, CX - 1] - coef[1, CX - 1] * x_hi
     total[...] = jnp.zeros_like(total)
 
     def plane(x, source):
-        halves = whole_plane(x, source, y_lo, y_hi, edge)
+        halves = whole_plane(x, s, source, y_a, y_b, edge)
         image[:, x, 0:8, :], image[:, x, 8:16, :] = halves
         pair = rows_of(split(slab(first_image, x)), split(side_by_side(halves)))
         total[...] += dot3(pair, split(slab(field, x)), True)
@@ -328,12 +354,6 @@
 
 def tall(matrix):
     return jnp.concatenate([matrix, jnp.zeros((112, 128), F32)], axis=0)
-
-
-def early_kernel(carried, out):
-    projection, curvature = carried[4:6], carried[6:8]
-    unit = (iota((16, 128), 0) == iota((16, 128), 1) - 32).astype(F32)
-    out[...] = eliminate(unpack(curvature, 0) + unpack(projection, 16) + unit)
 
 
 def finish_kernel(
@@ -413,10 +433,16 @@
     return lax.all_to_all(pieces, axes, split_axis=0, concat_axis=0, tiled=True)
 
 
-def swap_edges(low, high, axes):
-    count = lax.axis_size(axes)
-    up = [(i, (i + 1) % count) for i in range(count)]
-    return lax.ppermute(high, axes, up), lax.ppermute(low, axes, [(b, a) for a, b in up])
+def swap_edges(x_a, x_b, y_a, y_b):
+    def swap(array, axes, first):
+        count = lax.axis_size(axes)
+        partner = [i + 1 if i % 2 == first else i - 1 for i in range(count)]
+        pairs = [(i, p if 0 <= p < count else i) for i, p in enumerate(partner)]
+        return lax.ppermute(array, axes, pairs)
+
+    y_b, x_b = swap(y_b, SUB, 1), swap(x_b, GRP, 1)
+    x_a, y_a = swap(x_a, GRP, 0), swap(y_a, SUB, 0)
+    return x_a, x_b, y_a, y_b
 
 
 def copy_sems(count):
@@ -437,7 +463,7 @@
         return exchange(partial, GRP)
 
     def precondition(pieces, field):
-        smoothed, x_lo, x_hi, y_lo, y_hi, carried = call(
+        smoothed, *edges, carried = call(
             prolong_kernel,
             [FIELD, face, face, face, face, tile],
             [bases, FIELD, copy_sems(2)],
@@ -449,12 +475,13 @@
             far=(1, 2),
             limit=PROLONG_LIMIT,
         )
-        edges = (*swap_edges(x_lo, x_hi, GRP), *swap_edges(y_lo, y_hi, SUB))
-        (inner,) = call(inner_kernel, [FIELD], [], smoothed, coef)
-        return smoothed, (inner, *edges, coef, edge), carried
-
-    x_edges = swap_edges(conductivity[0], conductivity[-1], GRP)
-    y_edges = swap_edges(conductivity[:, 0], conductivity[:, -1], SUB)
+        return smoothed, swap_edges(*edges), carried
+
+    g, s = position()
+    ends = (
+        *in_order(g, conductivity[-1], conductivity[0]),
+        *in_order(s, conductivity[:, -1], conductivity[:, 0]),
+    )
     (pieces,) = call(
         restrict_kernel,
         [(N_SUB, *tile)],
@@ -470,28 +497,37 @@
         [],
         conductivity,
         pinned_cells,
-        *x_edges,
-        *y_edges,
-    )
-    first, inner, _ = precondition(pieces, right_side)
+        *swap_edges(*ends),
+    )
+    pieces, scaling, keep, coef, edge = lax.optimization_barrier(
+        (pieces, scaling, keep, coef, edge)
+    )
+    first, edges, _ = precondition(pieces, right_side)
+    (inner,) = call(inner_kernel, [FIELD], [], first, coef)
     first_image, pieces = call(
         first_image_kernel,
         [FIELD, (N_SUB, *tile)],
         [FIELD, (VEC * 8 + 128, 128), (128, 128), bases, FIELD, copy_sems(1), copy_sems(2)],
-        *inner,
+        inner,
+        *edges,
+        coef,
+        edge,
         first,
         coarse_basis,
         right_side,
         far=(8, 9, 10),
         limit=IMAGE_LIMIT,
     )
-    second, inner, carried = precondition(pieces, first_image)
-    (early,) = call(early_kernel, [(16, 128)], [], carried)
+    second, edges, carried = precondition(pieces, first_image)
+    inner, early = call(inner_and_early_kernel, [FIELD, (16, 128)], [], second, coef, carried)
     second_image, pieces = call(
         second_image_kernel,
         [FIELD, (N_GRP, *tile)],
         [FIELD, (256, 128), FIELD, copy_sems(1), copy_sems(1)],
-        *inner,
+        inner,
+        *edges,
+        coef,
+        edge,
         second,
         first_image,
         far=(8, 9),

time: 160 us -> 161 us (level)
  blocking collectives: 38.3 us -> 91.4 us
  starting transfers between devices: 46.6 us -> 19.9 us
  waiting for transfers between devices: 27.4 us -> 3.16 us
    all_to_all x3 -> x6, blocking collectives: 38.3 us -> 91.4 us  [exchange(): return lax.all_to_all(pieces, axes, split_axis=0, concat_axis=0, tiled=True)]
    all_to_all x3 -> x0, starting transfers between devices: 29.3 us -> none  [exchange(): return lax.all_to_all(pieces, axes, split_axis=0, concat_axis=0, tiled=True)]
    all_to_all x3 -> x0, waiting for transfers between devices: 17.8 us -> none  [exchange(): return lax.all_to_all(pieces, axes, split_axis=0, concat_axis=0, tiled=True)]
    ppermute x12, waiting for transfers between devices: 9.56 us -> 3.16 us  [swap(): return lax.ppermute(array, axes, pairs)]
    ppermute x12, starting transfers between devices: 17.3 us -> 19.9 us  [swap(): return lax.ppermute(array, axes, pairs)]
    pallas_call x13 -> x12, Pallas kernels: 41.8 us -> 40.3 us  [call(): pl.pallas_call(kernel, out_shape=[jax.ShapeDtypeStruct(shape, F32) for sh...]
    unnamed x22 -> x18, local copies, waits for them, and re-layouts: 4.05 us -> 2.76 us
  transfers between devices with their start and end apart: 15 -> 12, of which waited for: 7 -> 2; matrix products, arithmetic and copies ran while one was open for 0% -> 0% of each run, Pallas kernels for 4% -> 7%
where the time goes in v2:
time: 161 us; the launch traced here: 160 us
  blocking collectives  91.4 us (57%)
  Pallas kernels  40.3 us (25%)
  starting transfers between devices  19.9 us (12%)
  local copies, waits for them, and re-layouts  3.65 us (2%)
  waiting for transfers between devices  3.16 us (2%)
    all_to_all x6, blocking collectives, exchange(): return lax.all_to_all(pieces, axes, split_axis=0, concat_axis=0, tiled=True)  91.4 us
    pallas_call x12, Pallas kernels, call(): pl.pallas_call(kernel, out_shape=[jax.ShapeDtypeStruct(shape, F32) for sh...  40.3 us
    ppermute x12, starting transfers between devices, swap(): return lax.ppermute(array, axes, pairs)  19.9 us
  transfers between devices with their start and end apart: 12, of which 2 were waited for; matrix products, arithmetic and copies ran while one was open for 0% of the time, Pallas kernels for 7%

profile of v2, /device:TPU:1, one launch (start us, length us, event | category | flops | bytes accessed | tf_op | source)
XLA Modules:
  0.0 160.3 jit_solution(7034186939435290166)
XLA Ops:
  0.6 0.9 fusion
  1.6 4.5 %collective-permute-start.3 = (f32[16,128]{1,0:T(8,128)S(1)}, f32[16,128]{1,0:T(8,128)S(1)}, u32[]{:S(2)}, u32[]{:S(2)}) collective-permute-start(f32[16,128]{1,0:T(8,128)S(1)} %get-tuple-element.58), channel_id=1, source_target_pairs={{0,0},{1,2},{2,1},{3,4},{4,3},{5,6},{6,5},{7,8},{8,7},{9,10},{10,9... | collective-permute-start | bytes 24584 | tf_op jit(solution)/shard_map/ppermute | solution.py:441
  6.1 0.1 collective-permute-start.2
  6.2 0.7 select_bitcast_fusion.2
  6.9 0.6 collective-permute-start.1
  7.5 0.0 copy-start.5
  7.6 0.0 copy-start.6
  7.6 0.0 copy-start.3
  7.6 3.9 %collective-permute-start = (f32[16,128]{1,0:T(8,128)S(1)}, f32[16,128]{1,0:T(8,128)S(1)}, u32[]{:S(2)}, u32[]{:S(2)}) collective-permute-start(f32[16,128]{1,0:T(8,128)S(1)} %get-tuple-element.57), channel_id=1, source_target_pairs={{0,32},{32,0},{64,96},{96,64},{128,160},{160,128},{192,224},{224,1... | collective-permute-start | bytes 24584 | tf_op jit(solution)/shard_map/ppermute | solution.py:441
  11.5 5.9 %shard_map.68 = f32[32,8,128]{2,1,0:T(8,128)} custom-call(f32[32,16,16,128]{3,2,1,0:T(8,128)} %basis_hbm.7, f32[16,16,16,128]{3,2,1,0:T(8,128)} %right_side_hbm.3), custom_call_target="tpu_custom_call" | custom-call | tf_op jit(solution)/shard_map/pallas_call | solution.py:422
  17.4 0.0 collective-permute-done.3.y_b
  17.4 0.0 collective-permute-done.2.y_a
  17.4 0.0 collective-permute-done.1.x_b
  17.4 0.0 collective-permute-done.x_a
  17.4 0.0 copy-done.5
  17.4 0.0 copy-done.6
  17.4 0.3 shard_map.69
  17.7 23.2 %all_to_all.30.gathered = f32[32,8,128]{2,1,0:T(8,128)S(1)} all-to-all(f32[32,8,128]{2,1,0:T(8,128)} %shard_map.68), channel_id=1, replica_groups=mesh['grp_0'=2,'grp_1'=4,'sub_0'=4,'sub_1'=4,'sub_2'=2] {'sub_0','sub_1'..., dimensions={0} | all-to-all | bytes 262144 | tf_op jit(solution)/shard_map/all_to_all | solution.py:433
  40.9 0.0 copy-done.3
  40.9 1.0 shard_map.70
  41.9 7.9 %all_to_all.31.arrived = f32[8,8,128]{2,1,0:T(8,128)S(1)} all-to-all(f32[8,8,128]{2,1,0:T(8,128)S(1)} %shard_map.70), channel_id=1, replica_groups=mesh['grp_0'=2,'grp_1'=4,'sub_0'=4,'sub_1'=4,'sub_2'=2] {'grp_0','grp_1'}, dimensions={0} | all-to-all | bytes 65536 | tf_op jit(solution)/shard_map/all_to_all | solution.py:433
  49.7 3.5 %shard_map.71 = (f32[16,16,16,128]{3,2,1,0:T(8,128)S(1)}, f32[16,16,128]{2,1,0:T(8,128)S(1)}, f32[16,16,128]{2,1,0:T(8,128)S(1)}, f32[16,16,128]{2,1,0:T(8,128)S...) custom-call(f32[8,8,128]{2,1,0:T(8,128)S(1)} %all_to_all.31.arrived, f32[32,16,16,128]{3,2,1,0:T(8,128)} %basis_hbm.7, ...), custom_call_target="tpu_custom_call" | custom-call | tf_op jit(solution)/shard_map/pallas_call | solution.py:422
  53.2 0.0 copy-start.1
  53.2 0.4 collective-permute-start.4
  53.6 0.7 collective-permute-start.5
  54.2 2.1 %collective-permute-start.6 = (f32[16,16,128]{2,1,0:T(8,128)S(1)}, f32[16,16,128]{2,1,0:T(8,128)S(1)}, u32[]{:S(2)}, u32[]{:S(2)}) collective-permute-start(f32[16,16,128]{2,1,0:T(8,128)S(1)} %get-tuple-element.39), channel_id=1, source_target_pairs={{0,1},{1,0},{2,3},{3,2},{4,5},{5,4},{6,7},{7,6},{8,9},{9,8},{10,11... | collective-permute-start | bytes 393224 | tf_op jit(solution)/shard_map/ppermute | solution.py:441
  56.3 2.3 %collective-permute-start.7 = (f32[16,16,128]{2,1,0:T(8,128)S(1)}, f32[16,16,128]{2,1,0:T(8,128)S(1)}, u32[]{:S(2)}, u32[]{:S(2)}) collective-permute-start(f32[16,16,128]{2,1,0:T(8,128)S(1)} %get-tuple-element.40), channel_id=1, source_target_pairs={{0,0},{1,2},{2,1},{3,4},{4,3},{5,6},{6,5},{7,8},{8,7},{9,10},{10,9... | collective-permute-start | bytes 393224 | tf_op jit(solution)/shard_map/ppermute | solution.py:441
  58.6 1.7 %shard_map.72.inner = f32[16,16,16,128]{3,2,1,0:T(8,128)S(1)} custom-call(f32[16,16,16,128]{3,2,1,0:T(8,128)S(1)} %get-tuple-element.35.field.first_hbm, f32[7,16,16,128]{3,2,1,0:T(8,128)S(1)} %get-tuple-element.36.coef), custom_call_target="tpu_custom_call" | custom-call | tf_op jit(solution)/shard_map/pallas_call | solution.py:422
  60.3 0.0 collective-permute-done.4.x_a
  60.4 0.0 collective-permute-done.5.x_b
  60.4 0.0 collective-permute-done.6.y_a
  60.4 2.2 %collective-permute-done.7.y_b = f32[16,16,128]{2,1,0:T(8,128)S(1)} collective-permute-done((f32[16,16,128]{2,1,0:T(8,128)S(1)}, f32[16,16,128]{2,1,0:T(8,128)S(1)}, u32[]{:S(2)}, u32[]{:S(2)}) %collective-permute-start.7) | collective-permute-done | bytes 131104 | tf_op jit(solution)/shard_map/ppermute | solution.py:441
  62.6 0.0 copy-done.1
  62.6 7.4 %shard_map.73 = (f32[16,16,16,128]{3,2,1,0:T(8,128)S(1)}, f32[32,8,128]{2,1,0:T(8,128)S(1)}) custom-call(f32[16,16,16,128]{3,2,1,0:T(8,128)S(1)} %shard_map.72.inner, f32[16,16,128]{2,1,0:T(8,128)S(1)} %collective-permute-done.4.x_a, f32[16,16,128]{2,1,0:T(8,128)S(1)} %collective-permute-done.5.x_b, f32[16,16,128]{2,1,0:T(8,128)S(1)} %collective-permute-done.6.y_a, ...), custom_call_target="tpu_custom_call" | custom-call | tf_op jit(solution)/shard_map/pallas_call | solution.py:422
  70.0 0.0 copy-start
  70.0 1.3 copy-done
  71.3 17.8 %all_to_all.32.gathered = f32[32,8,128]{2,1,0:T(8,128)S(1)} all-to-all(f32[32,8,128]{2,1,0:T(8,128)S(1)} %get-tuple-element.42), channel_id=1, replica_groups=mesh['grp_0'=2,'grp_1'=4,'sub_0'=4,'sub_1'=4,'sub_2'=2] {'sub_0','sub_1'..., dimensions={0} | all-to-all | bytes 262144 | tf_op jit(solution)/shard_map/all_to_all | solution.py:433
  89.2 1.0 shard_map.74
  90.2 12.2 %all_to_all.33.arrived = f32[8,8,128]{2,1,0:T(8,128)S(1)} all-to-all(f32[8,8,128]{2,1,0:T(8,128)S(1)} %shard_map.74), channel_id=1, replica_groups=mesh['grp_0'=2,'grp_1'=4,'sub_0'=4,'sub_1'=4,'sub_2'=2] {'grp_0','grp_1'}, dimensions={0} | all-to-all | bytes 65536 | tf_op jit(solution)/shard_map/all_to_all | solution.py:433
  102.4 3.3 %shard_map.75 = (f32[16,16,16,128]{3,2,1,0:T(8,128)S(1)}, f32[16,16,128]{2,1,0:T(8,128)S(1)}, f32[16,16,128]{2,1,0:T(8,128)S(1)}, f32[16,16,128]{2,1,0:T(8,128)S...) custom-call(f32[8,8,128]{2,1,0:T(8,128)S(1)} %all_to_all.33.arrived, f32[32,16,16,128]{3,2,1,0:T(8,128)} %basis_hbm.7, ...), custom_call_target="tpu_custom_call" | custom-call | tf_op jit(solution)/shard_map/pallas_call | solution.py:422
  105.6 0.0 copy-start.2
  105.6 0.0 copy-start.7
  105.7 0.4 collective-permute-start.8
  106.0 0.7 collective-permute-start.9
  106.7 2.1 %collective-permute-start.10 = (f32[16,16,128]{2,1,0:T(8,128)S(1)}, f32[16,16,128]{2,1,0:T(8,128)S(1)}, u32[]{:S(2)}, u32[]{:S(2)}) collective-permute-start(f32[16,16,128]{2,1,0:T(8,128)S(1)} %get-tuple-element.49), channel_id=1, source_target_pairs={{0,1},{1,0},{2,3},{3,2},{4,5},{5,4},{6,7},{7,6},{8,9},{9,8},{10,11... | collective-permute-start | bytes 393224 | tf_op jit(solution)/shard_map/ppermute | solution.py:441
  108.8 2.2 %collective-permute-start.11 = (f32[16,16,128]{2,1,0:T(8,128)S(1)}, f32[16,16,128]{2,1,0:T(8,128)S(1)}, u32[]{:S(2)}, u32[]{:S(2)}) collective-permute-start(f32[16,16,128]{2,1,0:T(8,128)S(1)} %get-tuple-element.50), channel_id=1, source_target_pairs={{0,0},{1,2},{2,1},{3,4},{4,3},{5,6},{6,5},{7,8},{8,7},{9,10},{10,9... | collective-permute-start | bytes 393224 | tf_op jit(solution)/shard_map/ppermute | solution.py:441
  111.0 3.1 %shard_map.76 = (f32[16,16,16,128]{3,2,1,0:T(8,128)S(1)}, f32[16,128]{1,0:T(8,128)S(1)}) custom-call(f32[16,16,16,128]{3,2,1,0:T(8,128)S(1)} %get-tuple-element.44.field.second_hbm, f32[7,16,16,128]{3,2,1,0:T(8,128)S(1)} %get-tuple-element.36.coef, f32[8,128]{1,0:T(8,128)S(1)} %get-tuple-element.45.carried), custom_call_target="tpu_custom_call" | custom-call | tf_op jit(solution)/shard_map/pallas_call | solution.py:422
  114.1 0.0 copy-start.8
  114.1 0.0 collective-permute-done.8.x_a
  114.1 0.0 collective-permute-done.9.x_b
  114.1 0.0 collective-permute-done.10.y_a
  114.1 0.9 collective-permute-done.11.y_b
  115.0 5.1 %shard_map.77 = (f32[16,16,16,128]{3,2,1,0:T(8,128)S(1)}, f32[8,8,128]{2,1,0:T(8,128)S(1)}) custom-call(f32[16,16,16,128]{3,2,1,0:T(8,128)S(1)} %get-tuple-element.46.inner, f32[16,16,128]{2,1,0:T(8,128)S(1)} %collective-permute-done.8.x_a, f32[16,16,128]{2,1,0:T(8,128)S(1)} %collective-permute-done.9.x_b, f32[16,16,128]{2,1,0:T(8,128)S(1)} %collective-permute-done.10.y_a, ...), custom_call_target="tpu_custom_call" | custom-call | tf_op jit(solution)/shard_map/pallas_call | solution.py:422
  120.1 0.0 copy-done.2
  120.1 0.0 copy-done.7
  120.2 0.0 copy-done.8
  120.2 0.0 copy-start.4
  120.2 1.4 copy-done.4
  121.6 10.7 %all_to_all.34.arrived = f32[8,8,128]{2,1,0:T(8,128)S(1)} all-to-all(f32[8,8,128]{2,1,0:T(8,128)S(1)} %get-tuple-element.51), channel_id=1, replica_groups=mesh['grp_0'=2,'grp_1'=4,'sub_0'=4,'sub_1'=4,'sub_2'=2] {'grp_0','grp_1'}, dimensions={0} | all-to-all | bytes 65536 | tf_op jit(solution)/shard_map/all_to_all | solution.py:433
  132.3 19.7 %all_to_all.35.arrived = f32[32,8,128]{2,1,0:T(8,128)} all-to-all(f32[32,8,128]{2,1,0:T(8,128)S(1)} %shard_map.78), channel_id=1, replica_groups=mesh['grp_0'=2,'grp_1'=4,'sub_0'=4,'sub_1'=4,'sub_2'=2] {'sub_0','sub_1'..., dimensions={0} | all-to-all | bytes 262144 | tf_op jit(solution)/shard_map/all_to_all | solution.py:433
  152.0 8.1 %shard_map.79 = (f32[16,16,16,128]{3,2,1,0:T(8,128)}, f32[16,16,16,128]{3,2,1,0:T(8,128)}) custom-call(f32[32,8,128]{2,1,0:T(8,128)} %all_to_all.35.arrived, f32[8,128]{1,0:T(8,128)} %copy-done.7, f32[16,128]{1,0:T(8,128)} %copy-done.8, f32[16,16,16,128]{3,2,1,0:T(8,128)} %copy-done.1, f32[16,16,16,128]{3,2,1,0:T(8,128)} %copy-done.2, ...), custom_call_target="tpu_custom_call" | custom-call | tf_op jit(solution)/shard_map/pallas_call | solution.py:422
  (2 shorter events, 0.0 us)
Async XLA Ops:
  1.6 15.8 %collective-permute-start.3 = (f32[16,128]{1,0:T(8,128)S(1)}, f32[16,128]{1,0:T(8,128)S(1)}, u32[]{:S(2)}, u32[]{:S(2)}) collective-permute-start(f32[16,128]{1,0:T(8,128)S(1)} %get-tuple-element.58), channel_id=1, source_target_pairs={{0,0},{1,2},{2,1},{3,4},{4,3},{5,6},{6,5},{7,8},{8,7},{9,10},{10,9... | collective-permute-start | bytes 24584 | tf_op jit(solution)/shard_map/ppermute | solution.py:441
  6.1 11.3 %collective-permute-start.2 = (f32[16,128]{1,0:T(8,128)S(1)}, f32[16,128]{1,0:T(8,128)S(1)}, u32[]{:S(2)}, u32[]{:S(2)}) collective-permute-start(f32[16,128]{1,0:T(8,128)S(1)} %get-tuple-element.59), channel_id=1, source_target_pairs={{0,1},{1,0},{2,3},{3,2},{4,5},{5,4},{6,7},{7,6},{8,9},{9,8},{10,11... | collective-permute-start | bytes 24584 | tf_op jit(solution)/shard_map/ppermute | solution.py:441
  6.9 10.5 %collective-permute-start.1 = (f32[16,128]{1,0:T(8,128)S(1)}, f32[16,128]{1,0:T(8,128)S(1)}, u32[]{:S(2)}, u32[]{:S(2)}) collective-permute-start(f32[16,128]{1,0:T(8,128)S(1)} %get-tuple-element.56), channel_id=1, source_target_pairs={{0,0},{32,64},{64,32},{96,128},{128,96},{160,192},{192,160},{224,2... | collective-permute-start | bytes 24584 | tf_op jit(solution)/shard_map/ppermute | solution.py:441
  7.5 9.9 %copy-start.5 = (f32[16,16,128]{2,1,0:T(8,128)S(1)}, f32[16,16,128]{2,1,0:T(8,128)}, u32[]{:S(2)}) copy-start(f32[16,16,128]{2,1,0:T(8,128)} %cond.1) | copy-start | bytes 393220
  7.6 9.9 %copy-start.6 = (s32[16,16,128]{2,1,0:T(8,128)S(1)}, s32[16,16,128]{2,1,0:T(8,128)}, u32[]{:S(2)}) copy-start(s32[16,16,128]{2,1,0:T(8,128)} %pinned.1) | copy-start | bytes 393220
  7.6 33.3 %copy-start.3 = (f32[8,32,1024]{2,1,0:T(8,128)S(1)}, f32[8,32,1024]{2,1,0:T(8,128)}, u32[]{:S(2)}) copy-start(f32[8,32,1024]{2,1,0:T(8,128)} %inverse.3) | copy-start | bytes 3145732
  7.6 9.8 %collective-permute-start = (f32[16,128]{1,0:T(8,128)S(1)}, f32[16,128]{1,0:T(8,128)S(1)}, u32[]{:S(2)}, u32[]{:S(2)}) collective-permute-start(f32[16,128]{1,0:T(8,128)S(1)} %get-tuple-element.57), channel_id=1, source_target_pairs={{0,32},{32,0},{64,96},{96,64},{128,160},{160,128},{192,224},{224,1... | collective-permute-start | bytes 24584 | tf_op jit(solution)/shard_map/ppermute | solution.py:441
  53.2 9.4 %copy-start.1 = (f32[16,16,16,128]{3,2,1,0:T(8,128)}, f32[16,16,16,128]{3,2,1,0:T(8,128)S(1)}, u32[]{:S(2)}) copy-start(f32[16,16,16,128]{3,2,1,0:T(8,128)S(1)} %get-tuple-element.35.field.first_hbm) | copy-start | bytes 6291460
  53.2 7.1 %collective-permute-start.4 = (f32[16,16,128]{2,1,0:T(8,128)S(1)}, f32[16,16,128]{2,1,0:T(8,128)S(1)}, u32[]{:S(2)}, u32[]{:S(2)}) collective-permute-start(f32[16,16,128]{2,1,0:T(8,128)S(1)} %get-tuple-element.37), channel_id=1, source_target_pairs={{0,32},{32,0},{64,96},{96,64},{128,160},{160,128},{192,224},{224,1... | collective-permute-start | bytes 393224 | tf_op jit(solution)/shard_map/ppermute | solution.py:441
  53.6 6.8 %collective-permute-start.5 = (f32[16,16,128]{2,1,0:T(8,128)S(1)}, f32[16,16,128]{2,1,0:T(8,128)S(1)}, u32[]{:S(2)}, u32[]{:S(2)}) collective-permute-start(f32[16,16,128]{2,1,0:T(8,128)S(1)} %get-tuple-element.38), channel_id=1, source_target_pairs={{0,0},{32,64},{64,32},{96,128},{128,96},{160,192},{192,160},{224,2... | collective-permute-start | bytes 393224 | tf_op jit(solution)/shard_map/ppermute | solution.py:441
  54.2 6.1 %collective-permute-start.6 = (f32[16,16,128]{2,1,0:T(8,128)S(1)}, f32[16,16,128]{2,1,0:T(8,128)S(1)}, u32[]{:S(2)}, u32[]{:S(2)}) collective-permute-start(f32[16,16,128]{2,1,0:T(8,128)S(1)} %get-tuple-element.39), channel_id=1, source_target_pairs={{0,1},{1,0},{2,3},{3,2},{4,5},{5,4},{6,7},{7,6},{8,9},{9,8},{10,11... | collective-permute-start | bytes 393224 | tf_op jit(solution)/shard_map/ppermute | solution.py:441
  56.3 6.3 %collective-permute-start.7 = (f32[16,16,128]{2,1,0:T(8,128)S(1)}, f32[16,16,128]{2,1,0:T(8,128)S(1)}, u32[]{:S(2)}, u32[]{:S(2)}) collective-permute-start(f32[16,16,128]{2,1,0:T(8,128)S(1)} %get-tuple-element.40), channel_id=1, source_target_pairs={{0,0},{1,2},{2,1},{3,4},{4,3},{5,6},{6,5},{7,8},{8,7},{9,10},{10,9... | collective-permute-start | bytes 393224 | tf_op jit(solution)/shard_map/ppermute | solution.py:441
  70.0 1.3 copy-start
  105.6 14.5 %copy-start.2 = (f32[16,16,16,128]{3,2,1,0:T(8,128)}, f32[16,16,16,128]{3,2,1,0:T(8,128)S(1)}, u32[]{:S(2)}) copy-start(f32[16,16,16,128]{3,2,1,0:T(8,128)S(1)} %get-tuple-element.44.field.second_hbm) | copy-start | bytes 6291460
  105.6 14.5 %copy-start.7 = (f32[8,128]{1,0:T(8,128)}, f32[8,128]{1,0:T(8,128)S(1)}, u32[]{:S(2)}) copy-start(f32[8,128]{1,0:T(8,128)S(1)} %get-tuple-element.45.carried) | copy-start | bytes 12292
  105.7 8.4 %collective-permute-start.8 = (f32[16,16,128]{2,1,0:T(8,128)S(1)}, f32[16,16,128]{2,1,0:T(8,128)S(1)}, u32[]{:S(2)}, u32[]{:S(2)}) collective-permute-start(f32[16,16,128]{2,1,0:T(8,128)S(1)} %get-tuple-element.47), channel_id=1, source_target_pairs={{0,32},{32,0},{64,96},{96,64},{128,160},{160,128},{192,224},{224,1... | collective-permute-start | bytes 393224 | tf_op jit(solution)/shard_map/ppermute | solution.py:441
  106.0 8.1 %collective-permute-start.9 = (f32[16,16,128]{2,1,0:T(8,128)S(1)}, f32[16,16,128]{2,1,0:T(8,128)S(1)}, u32[]{:S(2)}, u32[]{:S(2)}) collective-permute-start(f32[16,16,128]{2,1,0:T(8,128)S(1)} %get-tuple-element.48), channel_id=1, source_target_pairs={{0,0},{32,64},{64,32},{96,128},{128,96},{160,192},{192,160},{224,2... | collective-permute-start | bytes 393224 | tf_op jit(solution)/shard_map/ppermute | solution.py:441
  106.7 7.4 %collective-permute-start.10 = (f32[16,16,128]{2,1,0:T(8,128)S(1)}, f32[16,16,128]{2,1,0:T(8,128)S(1)}, u32[]{:S(2)}, u32[]{:S(2)}) collective-permute-start(f32[16,16,128]{2,1,0:T(8,128)S(1)} %get-tuple-element.49), channel_id=1, source_target_pairs={{0,1},{1,0},{2,3},{3,2},{4,5},{5,4},{6,7},{7,6},{8,9},{9,8},{10,11... | collective-permute-start | bytes 393224 | tf_op jit(solution)/shard_map/ppermute | solution.py:441
  108.8 6.3 %collective-permute-start.11 = (f32[16,16,128]{2,1,0:T(8,128)S(1)}, f32[16,16,128]{2,1,0:T(8,128)S(1)}, u32[]{:S(2)}, u32[]{:S(2)}) collective-permute-start(f32[16,16,128]{2,1,0:T(8,128)S(1)} %get-tuple-element.50), channel_id=1, source_target_pairs={{0,0},{1,2},{2,1},{3,4},{4,3},{5,6},{6,5},{7,8},{8,7},{9,10},{10,9... | collective-permute-start | bytes 393224 | tf_op jit(solution)/shard_map/ppermute | solution.py:441
  114.1 6.1 %copy-start.8 = (f32[16,128]{1,0:T(8,128)}, f32[16,128]{1,0:T(8,128)S(1)}, u32[]{:S(2)}) copy-start(f32[16,128]{1,0:T(8,128)S(1)} %get-tuple-element.52.early) | copy-start | bytes 24580
  120.2 1.4 copy-start.4
